TPU v7x, 512 devices: a whole 4x4x16 slice. The times are simulated.
512 devices in a mesh: dfa: 32 (over y, x, z_hi), hid: 16 (over z_lo, core).
Axes of the slice: x: 4, y: 4, z: 16 (z_hi: 2, z_lo: 8; z = z_hi * 8 + z_lo), core: 2. Of those that a mesh axis runs over, the one named last changes fastest.
Arguments:
- beta_last: bfloat16 [256, 32, 16, 64], P('dfa', None, 'hid'), may hold values from -6 to 6
- transition: bfloat16 [32, 16, 64, 32768], P(None, 'hid', None, 'dfa'), may hold values from -0.03125 to 0.03125
- emission: bfloat16 [64, 16, 2048], P(None, 'hid'), may hold values from 0.049804688 to 0.59765625
- successor: int32 [256, 8], replicated, may hold values from 0 to 255
- token_set: int32 [256, 8], replicated, may hold values from 0 to 63
Outputs:
- table: bfloat16 [2, 256, 32, 16, 64], P(None, 'dfa', None, 'hid')
All inputs are finite; a program needn't handle non-finite values.
Results may differ from a plain program's by a relative error of at most 0.0056.
Values may be sent and summed in bfloat16 or wider, within the bound.
No kernel may reach another device: no remote copies, remote signals or barrier semaphores. Data moves between devices by JAX's collectives and lax.ppermute only.
A program may use at most 128 MiB of HBM per device.

v0:
```python
import jax
import jax.numpy as jnp
from jax import lax
from jax.sharding import PartitionSpec as P

POS = 2


def edge_mix(full_cols, emission_rows, succ_rows, set_rows):
    width = full_cols.shape[0]
    count = succ_rows.shape[0]
    nsets = emission_rows.shape[0]
    total = jnp.zeros((width, count), jnp.float32)
    for column in range(succ_rows.shape[1]):
        picked = jnp.take(full_cols, succ_rows[:, column], axis=1)
        one_hot = (
            lax.broadcasted_iota(jnp.int32, (nsets, count), 0) == set_rows[:, column][None, :]
        ).astype(jnp.bfloat16)
        weights = lax.dot_general(
            emission_rows, one_hot, (((0,), (0,)), ((), ())), preferred_element_type=jnp.float32
        )
        total = total + weights * picked.astype(jnp.float32)
    return total.astype(jnp.bfloat16)


def local(beta_last, transition, emission, successor, token_set):
    state_count = beta_last.shape[0]
    block_count = beta_last.shape[1]
    cell_count = beta_last.shape[3]
    width = block_count * cell_count
    beta_cols = beta_last.reshape(state_count, width).T
    trans_block = transition.reshape(width, transition.shape[3])
    emission_rows = emission.reshape(emission.shape[0], width)
    results = []
    for position in range(POS):
        full_cols = lax.all_gather(beta_cols, "dfa", axis=1, tiled=True)
        first_row = lax.axis_index("dfa") * state_count
        succ_own = lax.dynamic_slice_in_dim(successor, first_row, state_count, 0)
        set_own = lax.dynamic_slice_in_dim(token_set, first_row, state_count, 0)
        own_cols = edge_mix(full_cols, emission_rows, succ_own, set_own)
        mixed_cols = lax.all_gather(own_cols, "dfa", axis=1, tiled=True)
        summed = lax.psum_scatter(
            lax.dot_general(
                trans_block,
                mixed_cols,
                (((0,), (0,)), ((), ())),
                preferred_element_type=jnp.float32,
            ),
            "hid",
            scatter_dimension=0,
            tiled=True,
        )
        beta_cols = lax.all_to_all(
            summed.astype(jnp.bfloat16), "dfa", split_axis=1, concat_axis=0, tiled=True
        )
        results = [beta_cols.T.reshape(state_count, block_count, 1, cell_count)] + results
    return jnp.stack(results)


def solution(mesh):
    return jax.shard_map(
        local,
        mesh=mesh,
        in_specs=(
            P("dfa", None, "hid", None),
            P(None, "hid", None, "dfa"),
            P(None, "hid", None),
            P(),
            P(),
        ),
        out_specs=P(None, "dfa", None, "hid", None),
        check_vma=False,
    )
```

profile of v0, /device:TPU:2, one launch (start us, length us, event | category | flops | bytes accessed | tf_op | source)
XLA Modules:
  0.0 713.5 jit_solution(4217858540283520598)
XLA Ops:
  6.5 0.0 all-gather.5.cloned.1.call-start
  6.5 1.6 reshape.29
  8.2 0.0 all-gather.5.cloned.1.call-update
  8.2 0.0 all-gather.7.cloned.1.call-start
  8.2 0.8 constant_dynamic-slice_fusion
  9.2 0.2 convolution_bitcast_fusion.7
  9.4 0.2 convolution_bitcast_fusion.1
  9.6 0.2 convolution_bitcast_fusion.2
  9.8 0.2 convolution_bitcast_fusion.3
  10.0 0.2 convolution_bitcast_fusion.4
  10.2 0.2 convolution_bitcast_fusion.5
  10.4 0.2 convolution_bitcast_fusion.6
  10.7 116.1 %all-gather.5.cloned.1.call-done = bf16[2048,256]{0,1:T(8,128)(2,1)} async-done(((bf16[2048,8]{0,1:T(8,128)(2,1)}), bf16[2048,256]{0,1:T(8,128)(2,1)}) %all-gather.5.cloned.1.call-update) | async-done | bytes 1048592 | tf_op jit(solution)/shard_map/all_gather | solution.py:36
  126.7 2.1 gather_fusion.7
  128.8 0.6 gather_fusion.6
  129.4 0.6 gather_fusion.5
  130.0 0.6 gather_fusion.4
  130.5 0.6 gather_fusion.3
  131.1 0.6 gather_fusion.2
  131.7 0.6 gather_fusion.1
  132.3 0.6 gather_fusion
  132.9 0.8 add_convert_fusion.1
  133.7 0.0 all-gather.7.cloned.1.call-update
  133.7 0.0 reduce-scatter.7.cloned.1.call-start
  133.8 100.9 %all-gather.7.cloned.1.call-done = bf16[2048,256]{0,1:T(8,128)(2,1)} async-done(((bf16[2048,8]{0,1:T(8,128)(2,1)}), bf16[2048,256]{0,1:T(8,128)(2,1)}) %all-gather.7.cloned.1.call-update) | async-done | bytes 1048592 | tf_op jit(solution)/shard_map/all_gather | solution.py:41
  234.7 3.8 convolution_bitcast_fusion.9
  238.4 1.3 copy.20
  239.8 0.0 reduce-scatter.7.cloned.1.call-update
  239.8 0.0 all-gather.9.cloned.1.call-start
  239.8 96.3 %reduce-scatter.7.cloned.1.call-done = f32[64,256]{1,0:T(8,128)} async-done(((f32[1024,256]{1,0:T(8,128)}), f32[64,256]{1,0:T(8,128)}) %reduce-scatter.7.cloned.1.call-update) | async-done | bytes 65552
  336.1 0.9 copy.21
  337.1 0.1 reshape.211
  337.2 25.9 %all_to_all.38 = bf16[32,2,256]{2,1,0:T(2,128)(2,1)S(1)} all-to-all(bf16[32,2,256]{2,1,0:T(2,128)(2,1)S(1)} %reshape.211), channel_id=1, replica_groups=mesh['dfa'=32,'hid'=16] {'dfa'}, dimensions={0} | all-to-all | bytes 65536 | tf_op jit(solution)/shard_map/all_to_all | solution.py:53
  363.1 0.1 reshape.212
  363.2 0.7 all_to_all.31
  364.0 0.0 all-gather.9.cloned.1.call-update
  364.0 0.0 all-gather.11.cloned.1.call-start
  364.0 104.5 %all-gather.9.cloned.1.call-done = bf16[2048,256]{0,1:T(8,128)(2,1)} async-done(((bf16[2048,8]{0,1:T(8,128)(2,1)}), bf16[2048,256]{0,1:T(8,128)(2,1)}) %all-gather.9.cloned.1.call-update) | async-done | bytes 1048592 | tf_op jit(solution)/shard_map/all_gather | solution.py:36
  468.5 2.1 gather_fusion.15
  470.6 0.6 gather_fusion.14
  471.1 0.6 gather_fusion.13
  471.7 0.6 gather_fusion.12
  472.3 0.6 gather_fusion.11
  472.9 0.6 gather_fusion.10
  473.5 0.6 gather_fusion.9
  474.0 0.6 gather_fusion.8
  474.6 0.8 add_convert_fusion
  475.4 0.0 all-gather.11.cloned.1.call-update
  475.4 0.0 copy-start.3
  475.4 0.0 reduce-scatter.9.cloned.1.call-start
  475.5 100.9 %all-gather.11.cloned.1.call-done = bf16[2048,256]{0,1:T(8,128)(2,1)} async-done(((bf16[2048,8]{0,1:T(8,128)(2,1)}), bf16[2048,256]{0,1:T(8,128)(2,1)}) %all-gather.11.cloned.1.call-update) | async-done | bytes 1048592 | tf_op jit(solution)/shard_map/all_gather | solution.py:41
  576.3 3.8 convolution_bitcast_fusion.8
  580.1 1.3 copy.22
  581.4 0.0 reduce-scatter.9.cloned.1.call-update
  581.4 96.5 %reduce-scatter.9.cloned.1.call-done = f32[64,256]{1,0:T(8,128)} async-done(((f32[1024,256]{1,0:T(8,128)}), f32[64,256]{1,0:T(8,128)}) %reduce-scatter.9.cloned.1.call-update) | async-done | bytes 65552
  677.9 0.9 copy.23
  678.9 0.7 reshape.213
  679.6 10.2 %all-to-all-start.1 = ((bf16[32,2,256]{2,1,0:T(2,128)(2,1)}), bf16[32,2,256]{2,1,0:T(2,128)(2,1)S(1)}, u32[]{:S(2)}, u32[]{:S(2)}) async-start(bf16[32,2,256]{2,1,0:T(2,128)(2,1)} %reshape.213), calls=%async_computation.1 | async-start | bytes 65536 | tf_op jit(solution)/shard_map/all_to_all | solution.py:53
  689.8 0.1 stack_reshape.7
  690.0 15.6 %all-to-all-done.1 = bf16[32,2,256]{2,1,0:T(2,128)(2,1)S(1)} async-done(((bf16[32,2,256]{2,1,0:T(2,128)(2,1)}), bf16[32,2,256]{2,1,0:T(2,128)(2,1)S(1)}, u32[]{:S(2)}, u32[]{:S(2)}) %all-to-all-start.1) | async-done | bytes 32800 | tf_op jit(solution)/shard_map/all_to_all | solution.py:53
  705.6 0.1 reshape.214
  705.7 0.1 all_to_all.35
  705.9 0.1 stack_reshape.6
  706.0 0.7 pad_maximum_fusion
  (23 shorter events, 0.1 us)
Async XLA Ops:
  6.5 2.6 copy-start
  6.5 120.2 %all-gather.5.cloned.1.call-start = ((), (), s32[]{:S(2)}) async-start(), calls=%async_computation.4 | async-start | bytes 1081344 | tf_op jit(solution)/shard_map/all_gather | solution.py:36
  8.2 226.5 %all-gather.7.cloned.1.call-start = ((), (), s32[]{:S(2)}) async-start(), calls=%async_computation.5 | async-start | bytes 1081344 | tf_op jit(solution)/shard_map/all_gather | solution.py:41
  126.7 2.1 copy-start.1
  133.7 202.3 %reduce-scatter.7.cloned.1.call-start = ((), (), s32[]{:S(2)}) async-start(), calls=%async_computation.8 | async-start | bytes 1114112
  239.8 228.7 %all-gather.9.cloned.1.call-start = ((), (), s32[]{:S(2)}) async-start(), calls=%async_computation.6 | async-start | bytes 1081344 | tf_op jit(solution)/shard_map/all_gather | solution.py:36
  364.0 212.3 %all-gather.11.cloned.1.call-start = ((), (), s32[]{:S(2)}) async-start(), calls=%async_computation.7 | async-start | bytes 1081344 | tf_op jit(solution)/shard_map/all_gather | solution.py:41
  468.5 2.1 copy-start.2
  475.4 214.4 %copy-start.3 = (bf16[2048,8]{0,1:T(8,128)(2,1)S(1)}, bf16[2048,8]{0,1:T(8,128)(2,1)}, u32[]{:S(2)}) copy-start(bf16[2048,8]{0,1:T(8,128)(2,1)} %all_to_all.31) | copy-start | bytes 98308
  475.4 202.5 %reduce-scatter.9.cloned.1.call-start = ((), (), s32[]{:S(2)}) async-start(), calls=%async_computation.9 | async-start | bytes 1114112
  679.6 26.0 %all-to-all-start.1 = ((bf16[32,2,256]{2,1,0:T(2,128)(2,1)}), bf16[32,2,256]{2,1,0:T(2,128)(2,1)S(1)}, u32[]{:S(2)}, u32[]{:S(2)}) async-start(bf16[32,2,256]{2,1,0:T(2,128)(2,1)} %reshape.213), calls=%async_computation.1 | async-start | bytes 65536 | tf_op jit(solution)/shard_map/all_to_all | solution.py:53
Sparse Core Ops, SparseCore 0:
  11.6 115.0 all-gather.4
  133.9 100.7 all-gather.6
  239.9 96.1 reduce-scatter.6
  364.1 104.3 all-gather.8
  475.5 100.7 all-gather.10
  581.6 96.2 reduce-scatter.8
where the time goes:
time: 714 us
  waiting for transfers between devices  631 us (88%)
  blocking collectives  25.9 us (4%)
  local copies, waits for them, and re-layouts  21.4 us (3%)
  between operations  13.8 us (2%)
  starting transfers between devices  10.4 us (1%)
  matrix products  9.82 us (1%)
    all_gather x2, waiting for transfers between devices, local(): full_cols = lax.all_gather(beta_cols, 'dfa', axis=1, tiled=True)  221 us
    all_gather x2, waiting for transfers between devices, local(): mixed_cols = lax.all_gather(own_cols, 'dfa', axis=1, tiled=True)  202 us
    unnamed x8, waiting for transfers between devices  193 us
    all_to_all x1, blocking collectives, local(): lax.all_to_all(summed.astype(jnp.bfloat16), 'dfa', split_axis=1, concat_a...  25.9 us
    all_to_all x1, waiting for transfers between devices, local(): lax.all_to_all(summed.astype(jnp.bfloat16), 'dfa', split_axis=1, concat_a...  15.6 us
  transfers between devices with their start and end apart: 7, of which 7 were waited for; matrix products, arithmetic and copies ran while one was open for 0% of the time, Pallas kernels for 0%

commit v1 on v0

v1 whole, which is shorter than its diff:
```python
import jax
import jax.numpy as jnp
from jax import lax
from jax.experimental import pallas as pl
from jax.experimental.pallas import tpu as pltpu
from jax.sharding import Mesh, PartitionSpec as P

BF, F32 = jnp.bfloat16, jnp.float32
DEG, NSET = 8, 64
PLANE = ("y", "x")
VMEM_LIMIT = 40 * 1024 * 1024


def dot(a, b):
    return jnp.dot(a, b, preferred_element_type=F32)


def one_hot_lanes(column, width):
    rows = column.shape[0]
    return (lax.broadcasted_iota(jnp.int32, (rows, width), 1) == column).astype(BF)


def one_hot_rows(row, height):
    cols = row.shape[1]
    return (lax.broadcasted_iota(jnp.int32, (height, cols), 0) == row).astype(BF)


def first_kernel(beta_ref, trans_ref, emis_ref, succ_ref, sets_ref, out_ref, pick, choose, total):
    step = pl.program_id(0)
    states = beta_ref.shape[0]

    @pl.when(step == 0)
    def _():
        total[...] = jnp.zeros_like(total)
        for j in range(DEG):
            pick[j] = one_hot_lanes(succ_ref[:, j : j + 1], states)
            choose[j] = one_hot_lanes(sets_ref[:, j : j + 1], NSET)

    mixed = jnp.zeros(beta_ref.shape, F32)
    for j in range(DEG):
        mixed = mixed + dot(choose[j], emis_ref[...]) * dot(pick[j], beta_ref[...])
    total[...] += dot(mixed.astype(BF), trans_ref[...])

    @pl.when(step == pl.num_programs(0) - 1)
    def _():
        half = out_ref.shape[0] // 2
        whole = total[...].T.reshape(-1, 2, 64, states)
        for c in range(2):
            out_ref[c * half : (c + 1) * half] = whole[:, c].reshape(half, states)


def mix_and_multiply(beta, trans, emis, succ, sets):
    states, width = beta.shape
    outs = trans.shape[1]
    blk = 256
    return pl.pallas_call(
        first_kernel,
        grid=(width // blk,),
        out_shape=jax.ShapeDtypeStruct((outs, states), F32),
        in_specs=[
            pl.BlockSpec((states, blk), lambda i: (0, i)),
            pl.BlockSpec((blk, outs), lambda i: (i, 0)),
            pl.BlockSpec((NSET, blk), lambda i: (0, i)),
            pl.BlockSpec((states, DEG), lambda i: (0, 0)),
            pl.BlockSpec((states, DEG), lambda i: (0, 0)),
        ],
        out_specs=pl.BlockSpec((outs, states), lambda i: (0, 0)),
        scratch_shapes=[
            pltpu.VMEM((DEG, states, states), BF),
            pltpu.VMEM((DEG, states, NSET), BF),
            pltpu.VMEM((states, outs), F32),
        ],
        compiler_params=pltpu.CompilerParams(vmem_limit_bytes=VMEM_LIMIT),
        name="mix_multiply",
    )(beta, trans, emis, succ, sets)


def middle_kernel(parts_ref, emis_ref, succ_ref, sets_ref, beta_ref, mixed_ref):
    total = parts_ref[0].astype(F32)
    for i in range(1, parts_ref.shape[0]):
        total = total + parts_ref[i].astype(F32)
    beta = total.astype(BF)
    beta_ref[...] = beta
    states = beta.shape[1]
    mixed = jnp.zeros(beta.shape, F32)
    for j in range(DEG):
        weights = dot(emis_ref[...], one_hot_rows(sets_ref[j : j + 1], NSET))
        mixed = mixed + weights * dot(beta, one_hot_rows(succ_ref[j : j + 1], states))
    mixed_ref[...] = mixed.astype(BF)


def sum_and_mix(parts, emis, succ, sets):
    shape = jax.ShapeDtypeStruct(parts.shape[1:], BF)
    return pl.pallas_call(
        middle_kernel,
        out_shape=(shape, shape),
        compiler_params=pltpu.CompilerParams(vmem_limit_bytes=VMEM_LIMIT),
        name="sum_mix",
    )(parts, emis, succ, sets)


def last_kernel(parts_ref, later_ref, out_ref):
    total = parts_ref[0].astype(F32)
    for i in range(1, parts_ref.shape[0]):
        total = total + parts_ref[i].astype(F32)
    beta = total.astype(BF).astype(F32)
    out_ref[...] = jnp.concatenate([beta, later_ref[...].astype(F32)], 0).T.astype(BF)


def sum_and_join(parts, later):
    _, width, states = parts.shape
    return pl.pallas_call(
        last_kernel,
        out_shape=jax.ShapeDtypeStruct((states, 2 * width), BF),
        compiler_params=pltpu.CompilerParams(vmem_limit_bytes=VMEM_LIMIT),
        name="sum_join",
    )(parts, later)


def spread(x, axes, count):
    return lax.all_to_all(jnp.broadcast_to(x[None], (count,) + x.shape), axes, 0, 0)


def gather_states(x):
    pair = spread(x, "zh", 2)
    return spread(pair, PLANE, 16).reshape((-1,) + x.shape[1:])


def reduce_hid(partial):
    pair = lax.all_to_all(partial.reshape(2, 8, 64, -1), "c", 0, 0)
    mine = (pair[0] + pair[1]).astype(BF)
    return lax.all_to_all(mine, "zl", 0, 0)


def local(beta_last, transition, emission, successor, token_set):
    states, blocks, _, cells = beta_last.shape
    width = blocks * cells
    trans = transition.reshape(width, transition.shape[3])
    emis = emission.reshape(NSET, width)
    own = lax.axis_index("y") * 8 + lax.axis_index("x") * 2 + lax.axis_index("zh")
    emis_own = lax.dynamic_slice_in_dim(emis, own * cells, cells, 1).T
    succ_t, sets_t = successor.T, token_set.T

    beta = gather_states(beta_last.reshape(states, width))
    partial = mix_and_multiply(beta, trans, emis, successor, token_set)
    later, mixed = sum_and_mix(reduce_hid(partial), emis_own, succ_t, sets_t)
    mixed = gather_states(mixed)
    partial = lax.dot_general(trans, mixed, (((0,), (0,)), ((), ())), preferred_element_type=F32)
    partial = partial.reshape(8, 2, 64, -1).swapaxes(0, 1)
    joined = sum_and_join(reduce_hid(partial), later)
    moved = lax.all_to_all(joined.reshape(32, states, 2, cells), PLANE + ("zh",), 0, 0)
    return moved.transpose(2, 1, 0, 3).reshape(2, states, blocks, 1, cells)


def solution(mesh):
    fine = Mesh(mesh.devices.reshape(4, 4, 2, 8, 2), ("y", "x", "zh", "zl", "c"))
    dfa, hid = ("y", "x", "zh"), ("zl", "c")
    return jax.shard_map(
        local,
        mesh=fine,
        in_specs=(
            P(dfa, None, hid, None),
            P(None, hid, None, dfa),
            P(None, hid, None),
            P(),
            P(),
        ),
        out_specs=P(None, dfa, None, hid, None),
        check_vma=False,
    )
```

time: 714 us -> 179 us (0.25)
  the two profiles are of different devices: /device:TPU:2 before, /device:TPU:32 now
where the time goes in v1:
time: 179 us; the launch traced here: 178 us
  blocking collectives  112 us (63%)
  waiting for transfers between devices  29.8 us (17%)
  starting transfers between devices  13.3 us (7%)
  local copies, waits for them, and re-layouts  9.36 us (5%)
  Pallas kernels  9.08 us (5%)
  matrix products  3.45 us (2%)
    all_to_all x3, blocking collectives, spread(): lax.all_to_all(jnp.broadcast_to(x[None], (count,) + x.shape), axes, 0, 0)  60.3 us
    all_to_all x1, blocking collectives, reduce_hid(): return lax.all_to_all(mine, 'zl', 0, 0)  22.8 us
    all_to_all x1, blocking collectives, local(): lax.all_to_all(joined.reshape(32, states, 2, cells), PLANE + ('zh',), 0, 0)  20.2 us
    all_to_all x1, waiting for transfers between devices, reduce_hid(): return lax.all_to_all(mine, 'zl', 0, 0)  15.6 us
    all_to_all x1, waiting for transfers between devices, spread(): lax.all_to_all(jnp.broadcast_to(x[None], (count,) + x.shape), axes, 0, 0)  14.1 us
    all_to_all x2, blocking collectives, reduce_hid(): pair = lax.all_to_all(partial.reshape(2, 8, 64, -1), 'c', 0, 0)  9.15 us
    pallas_call x1, Pallas kernels, mix_and_multiply(): pl.pallas_call(first_kernel, grid=(width // blk,), out_shape=jax.ShapeDty...  8.51 us
    all_to_all x1, starting transfers between devices, spread(): lax.all_to_all(jnp.broadcast_to(x[None], (count,) + x.shape), axes, 0, 0)  7.03 us
  transfers between devices with their start and end apart: 2, of which 2 were waited for; matrix products, arithmetic and copies ran while one was open for 1% of the time, Pallas kernels for 0%

profile of v1, /device:TPU:32, one launch (start us, length us, event | category | flops | bytes accessed | tf_op | source)
XLA Modules:
  0.0 178.3 jit_solution(6910330149321989381)
XLA Ops:
  0.0 1.0 broadcast_in_dim.10
  1.0 27.2 %all_to_all.45 = bf16[2,8,2048]{2,1,0:T(8,128)(2,1)S(1)} all-to-all(bf16[2,8,2048]{2,1,0:T(8,128)(2,1)S(1)} %broadcast_in_dim.11), channel_id=1, replica_groups=mesh['y'=4,'x'=4,'zh'=2,'zl'=8,'c'=2] {'zh'}, dimensions={0} | all-to-all | bytes 131072 | tf_op jit(solution)/shard_map/all_to_all | solution.py:121
  28.1 1.1 broadcast_in_dim.12
  29.2 7.0 %all-to-all-start.1 = ((bf16[16,2,8,2048]{3,2,1,0:T(8,128)(2,1)}), bf16[16,2,8,2048]{3,2,1,0:T(8,128)(2,1)S(1)}, u32[]{:S(2)}, u32[]{:S(2)}) async-start(bf16[16,2,8,2048]{3,2,1,0:T(8,128)(2,1)} %broadcast_in_dim.12), calls=%async_computation.1 | async-start | bytes 2097152 | tf_op jit(solution)/shard_map/all_to_all | solution.py:121
  36.3 0.8 copy.16.succ_ref
  37.1 0.8 copy.17.sets_ref
  37.9 14.1 %all-to-all-done.1 = bf16[16,2,8,2048]{3,2,1,0:T(8,128)(2,1)S(1)} async-done(((bf16[16,2,8,2048]{3,2,1,0:T(8,128)(2,1)}), bf16[16,2,8,2048]{3,2,1,0:T(8,128)(2,1)S(1)}, u32[]{:S(2)}, u32[]{:S(2)}) %all-to-all-start.1) | async-done | bytes 1048608 | tf_op jit(solution)/shard_map/all_to_all | solution.py:121
  52.0 0.0 copy-start
  52.0 2.2 %copy-done = bf16[32,1,64,1024]{3,2,1,0:T(8,128)(2,1)S(1)} copy-done((bf16[32,1,64,1024]{3,2,1,0:T(8,128)(2,1)S(1)}, bf16[32,1,64,1024]{3,2,1,0:T(8,128)(2,1)}, u32[]{:S(2)}) %copy-start) | copy-done | bytes 4194328
  54.2 0.0 copy-start.1
  54.2 0.9 copy-done.1
  55.2 0.0 copy-start.2
  55.2 0.0 copy-start.3
  55.2 8.5 %mix_multiply.1 = f32[1024,256]{1,0:T(8,128)S(1)} custom-call(bf16[256,2048]{1,0:T(8,128)(2,1)S(1)} %bitcast.37, bf16[2048,1024]{1,0:T(8,128)(2,1)S(1)} %bitcast.36, bf16[64,2048]{1,0:T(8,128)(2,1)S(1)} %bitcast.39, s32[256,8]{1,0:T(8,128)S(1)} %copy.16.succ_ref, s32[256,8]{1,0:T(8,128)S(1)} %copy.17.sets_ref), custom_call_target="tpu_custom_call" | custom-call | tf_op jit(solution)/shard_map/mix_multiply/pallas_call | solution.py:56
  63.7 4.6 %all_to_all.46 = f32[2,8,64,256]{3,2,1,0:T(8,128)S(1)} all-to-all(f32[2,8,64,256]{3,2,1,0:T(8,128)S(1)} %bitcast.38), channel_id=1, replica_groups=mesh['y'=4,'x'=4,'zh'=2,'zl'=8,'c'=2] {'c'}, dimensions={0} | all-to-all | bytes 2097152 | tf_op jit(solution)/shard_map/all_to_all | solution.py:130
  68.3 0.7 fusion.2
  69.0 6.3 %all-to-all-start.3 = ((bf16[8,64,256]{2,1,0:T(8,128)(2,1)}), bf16[8,64,256]{2,1,0:T(8,128)(2,1)S(1)}, u32[]{:S(2)}, u32[]{:S(2)}) async-start(bf16[8,64,256]{2,1,0:T(8,128)(2,1)} %fusion.2), calls=%async_computation.3 | async-start | bytes 524288 | tf_op jit(solution)/shard_map/all_to_all | solution.py:132
  75.3 0.8 constant_dynamic-slice_fusion
  76.1 0.1 copy.18
  76.2 15.6 %all-to-all-done.3.parts_ref = bf16[8,64,256]{2,1,0:T(8,128)(2,1)S(1)} async-done(((bf16[8,64,256]{2,1,0:T(8,128)(2,1)}), bf16[8,64,256]{2,1,0:T(8,128)(2,1)S(1)}, u32[]{:S(2)}, u32[]{:S(2)}) %all-to-all-start.3) | async-done | bytes 262176 | tf_op jit(solution)/shard_map/all_to_all | solution.py:132
  91.8 0.0 copy-done.2
  91.8 0.0 copy-done.3
  91.8 0.5 sum_mix.1
  92.3 15.5 %all_to_all.47 = bf16[2,64,256]{2,1,0:T(8,128)(2,1)S(1)} all-to-all(bf16[2,64,256]{2,1,0:T(8,128)(2,1)S(1)} %broadcast_in_dim.13), channel_id=1, replica_groups=mesh['y'=4,'x'=4,'zh'=2,'zl'=8,'c'=2] {'zh'}, dimensions={0} | all-to-all | bytes 131072 | tf_op jit(solution)/shard_map/all_to_all | solution.py:121
  107.8 0.1 broadcast_in_dim.14
  107.9 17.6 %all_to_all.48 = bf16[16,2,64,256]{3,2,1,0:T(8,128)(2,1)S(1)} all-to-all(bf16[16,2,64,256]{3,2,1,0:T(8,128)(2,1)S(1)} %broadcast_in_dim.14), channel_id=1, replica_groups=mesh['y'=4,'x'=4,'zh'=2,'zl'=8,'c'=2] {'y','x'}, dimensions={0} | all-to-all | bytes 2097152 | tf_op jit(solution)/shard_map/all_to_all | solution.py:121
  125.6 3.5 %convolution_bitcast_fusion = f32[1024,256]{0,1:T(8,128)S(1)} fusion(bf16[2048,256]{1,0:T(8,128)(2,1)S(1)} %bitcast.45, bf16[2048,1024]{1,0:T(8,128)(2,1)} %bitcast.35), kind=kOutput, calls=%fused_computation | convolution fusion | flops 1073741824 | bytes 6291456 | tf_op jit(solution)/shard_map/dot_general | solution.py:148
  129.0 0.3 copy.19
  129.3 0.1 copy.25
  129.4 4.6 %all_to_all.49 = f32[2,8,64,256]{3,2,1,0:T(8,128)S(1)} all-to-all(f32[2,8,64,256]{3,2,1,0:T(8,128)S(1)} %bitcast.44), channel_id=1, replica_groups=mesh['y'=4,'x'=4,'zh'=2,'zl'=8,'c'=2] {'c'}, dimensions={0} | all-to-all | bytes 2097152 | tf_op jit(solution)/shard_map/all_to_all | solution.py:130
  134.0 0.1 fusion.3
  134.1 22.8 %all_to_all.50.parts_ref = bf16[8,64,256]{2,1,0:T(8,128)(2,1)S(1)} all-to-all(bf16[8,64,256]{2,1,0:T(8,128)(2,1)S(1)} %fusion.3), channel_id=1, replica_groups=mesh['y'=4,'x'=4,'zh'=2,'zl'=8,'c'=2] {'zl'}, dimensions={0} | all-to-all | bytes 524288 | tf_op jit(solution)/shard_map/all_to_all | solution.py:132
  156.9 0.1 sum_join.1
  157.0 0.1 reshape.39
  157.1 0.1 reshape.41
  157.3 20.2 %all_to_all.51 = bf16[32,2,512]{2,1,0:T(2,128)(2,1)S(1)} all-to-all(bf16[32,2,512]{2,1,0:T(2,128)(2,1)S(1)} %reshape.41), channel_id=1, replica_groups=mesh['y'=4,'x'=4,'zh'=2,'zl'=8,'c'=2] {'y','x','zh'}, dimensions={0} | all-to-all | bytes 131072 | tf_op jit(solution)/shard_map/all_to_all | solution.py:151
  177.5 0.1 reshape.42
  177.6 0.7 copy.22
  (4 shorter events, 0.0 us)
Async XLA Ops:
  29.2 22.8 %all-to-all-start.1 = ((bf16[16,2,8,2048]{3,2,1,0:T(8,128)(2,1)}), bf16[16,2,8,2048]{3,2,1,0:T(8,128)(2,1)S(1)}, u32[]{:S(2)}, u32[]{:S(2)}) async-start(bf16[16,2,8,2048]{3,2,1,0:T(8,128)(2,1)} %broadcast_in_dim.12), calls=%async_computation.1 | async-start | bytes 2097152 | tf_op jit(solution)/shard_map/all_to_all | solution.py:121
  52.0 2.2 %copy-start = (bf16[32,1,64,1024]{3,2,1,0:T(8,128)(2,1)S(1)}, bf16[32,1,64,1024]{3,2,1,0:T(8,128)(2,1)}, u32[]{:S(2)}) copy-start(bf16[32,1,64,1024]{3,2,1,0:T(8,128)(2,1)} %param.6) | copy-start | bytes 12582916
  54.2 0.9 copy-start.1
  55.2 36.7 %copy-start.2 = (s32[256,8]{0,1:T(8,128)S(1)}, s32[256,8]{0,1:T(8,128)}, u32[]{:S(2)}) copy-start(s32[256,8]{0,1:T(8,128)} %param.8) | copy-start | bytes 24580
  55.2 36.7 %copy-start.3 = (s32[256,8]{0,1:T(8,128)S(1)}, s32[256,8]{0,1:T(8,128)}, u32[]{:S(2)}) copy-start(s32[256,8]{0,1:T(8,128)} %param.9) | copy-start | bytes 24580
  69.0 22.8 %all-to-all-start.3 = ((bf16[8,64,256]{2,1,0:T(8,128)(2,1)}), bf16[8,64,256]{2,1,0:T(8,128)(2,1)S(1)}, u32[]{:S(2)}, u32[]{:S(2)}) async-start(bf16[8,64,256]{2,1,0:T(8,128)(2,1)} %fusion.2), calls=%async_computation.3 | async-start | bytes 524288 | tf_op jit(solution)/shard_map/all_to_all | solution.py:132

commit v2 on v0

v2 whole, which is shorter than its diff:
```python
import jax
import jax.numpy as jnp
from jax import lax
from jax.experimental import pallas as pl
from jax.experimental.pallas import tpu as pltpu
from jax.sharding import Mesh, PartitionSpec as P

BF, F32 = jnp.bfloat16, jnp.float32
DEG, NSET = 8, 64
PLANE = ("y", "x")
MIB = 1024 * 1024
BLK = 256
BIG = 45
WHOLE = pl.BlockSpec(memory_space=pltpu.VMEM)
SCALAR = pl.BlockSpec(memory_space=pltpu.SMEM)


def shape(dims, dtype=BF):
    return jax.ShapeDtypeStruct(dims, dtype)


def params(mib):
    return pltpu.CompilerParams(vmem_limit_bytes=mib * MIB)


def dot(a, b, dims=((1,), (0,))):
    return lax.dot_general(a, b, (dims, ((), ())), preferred_element_type=F32)


ROWS = ((1,), (1,))


def iota(dims, axis):
    return lax.broadcasted_iota(jnp.int32, dims, axis)


def rows_kernel(beta_ref, out_ref):
    for i in range(0, beta_ref.shape[1], 2):
        out_ref[:, i * 64 : (i + 2) * 64] = jnp.concatenate([beta_ref[:, i], beta_ref[:, i + 1]], 1)


def as_rows(beta):
    states, blocks, cells = beta.shape
    return pl.pallas_call(
        rows_kernel, out_shape=shape((states, blocks * cells)), compiler_params=params(16), name="as_rows"
    )(beta)


def pair_kernel(zh_ref, mine_ref, theirs_ref, out_ref):
    mine, theirs = mine_ref[...].astype(F32), theirs_ref[...].astype(F32)
    first = zh_ref[0] == 0
    both = jnp.concatenate([jnp.where(first, mine, theirs), jnp.where(first, theirs, mine)], 0).astype(BF)
    for i in range(out_ref.shape[0]):
        out_ref[i] = both


def pair_copies(zh, mine, theirs):
    states, width = mine.shape
    return pl.pallas_call(
        pair_kernel,
        out_shape=shape((16, 2 * states, width)),
        in_specs=[SCALAR, WHOLE, WHOLE],
        compiler_params=params(16),
        name="pair_copies",
    )(zh, mine, theirs)


def first_kernel(
    plane_ref, beta_ref, succ_ref, sets_ref, emis_hbm, trans_hbm,
    out_ref, pick_ref, own_ref, flip_ref,
    emis_ref, trans, choose, total, arrived,
):
    emis_load = pltpu.make_async_copy(emis_hbm, emis_ref, arrived.at[0])
    trans_load = pltpu.make_async_copy(trans_hbm, trans, arrived.at[1])
    emis_load.start()
    trans_load.start()
    states, width = beta_ref.shape
    lanes = own_ref.shape[1]
    for j in range(DEG):
        at = slice(j * states, (j + 1) * states)
        pick_ref[at] = (iota((states, states), 1) == succ_ref[:, j : j + 1]).astype(BF)
        choose[at] = (iota((states, NSET), 1) == sets_ref[:, j : j + 1]).astype(BF)
    emis_load.wait()
    mine = emis_ref[:, pl.ds(pl.multiple_of(plane_ref[0] * lanes, lanes), lanes)].astype(F32).T.astype(BF)
    for j in range(DEG):
        own_ref[j] = dot(mine, choose[j * states : (j + 1) * states], ROWS).astype(BF)
    for b in range(width // BLK):
        cols = slice(b * BLK, (b + 1) * BLK)
        mixed = jnp.zeros((states, BLK), F32)
        for j in range(DEG):
            at = slice(j * states, (j + 1) * states)
            mixed = mixed + dot(pick_ref[at], beta_ref[:, cols]) * dot(choose[at], emis_ref[:, cols])
        if b == 0:
            trans_load.wait()
        flip_ref[b] = trans[cols].T
        part = dot(flip_ref[b], mixed.astype(BF), ROWS)
        total[...] = part if b == 0 else total[...] + part
    for i in range(4):
        for z in range(4):
            at = z * 4 + i
            out_ref[i, z * 64 : (z + 1) * 64] = total[at * 64 : (at + 1) * 64].astype(BF)


def mix_and_multiply(plane, beta, succ, sets, emis, trans):
    states = beta.shape[0]
    width, outs = trans.shape
    return pl.pallas_call(
        first_kernel,
        out_shape=(
            shape((4, outs // 4, states)),
            shape((DEG * states, states)),
            shape((DEG, 128, states)),
            shape((width // BLK, outs, BLK)),
        ),
        in_specs=[SCALAR] + [WHOLE] * 3 + [pl.BlockSpec(memory_space=pl.ANY)] * 2,
        out_specs=(WHOLE,) * 4,
        scratch_shapes=[
            pltpu.VMEM((NSET, width), BF),
            pltpu.VMEM((width, outs), BF),
            pltpu.VMEM((DEG * states, NSET), BF),
            pltpu.VMEM((outs, states), F32),
            pltpu.SemaphoreType.DMA((2,)),
        ],
        compiler_params=params(BIG),
        name="mix_multiply",
    )(plane, beta, succ, sets, emis, trans)


def near_kernel(parts_ref, out_ref):
    total = parts_ref[0].astype(F32)
    for i in range(1, 4):
        total = total + parts_ref[i].astype(F32)
    for i in range(2):
        out_ref[i] = total.astype(BF)


def near_sum(parts):
    _, rows, states = parts.shape
    return pl.pallas_call(
        near_kernel, out_shape=shape((2, rows, states)), compiler_params=params(16), name="near_sum"
    )(parts)


def half_place(states):
    return (states >> 3 & 1) * 128 + (states >> 4) * 8 + (states & 7)


def middle_kernel(zh_ref, parts_ref, pick_ref, own_ref, out_ref, keep_ref):
    pieces = []
    for s in range(2):
        total = parts_ref[4 * s].astype(F32)
        for i in range(1, 4):
            total = total + parts_ref[4 * s + i].astype(F32)
        pieces.append(total)
    beta = jnp.concatenate(pieces, 0).astype(BF)
    states = beta.shape[1]
    mixed = jnp.zeros(beta.shape, F32)
    for j in range(DEG):
        mixed = mixed + dot(beta, pick_ref[j * states : (j + 1) * states], ROWS) * own_ref[j].astype(F32)
    place = half_place(iota((states, states), 0))
    order = (iota((states, states), 1) == place).astype(BF)
    mixed = dot(mixed.astype(BF), order).astype(BF)
    for i in range(out_ref.shape[0]):
        out_ref[i] = mixed
    half = states // 2
    place = half_place(iota((states, half), 0)) - zh_ref[0] * half
    mine = (iota((states, half), 1) == place).astype(BF)
    keep_ref[...] = dot(beta, mine).astype(BF)


def sum_and_mix(zh, parts, pick, own):
    _, cells, states = parts.shape
    return pl.pallas_call(
        middle_kernel,
        out_shape=(shape((16, 2 * cells, states)), shape((2 * cells, states // 2))),
        in_specs=[SCALAR, WHOLE, WHOLE, WHOLE],
        compiler_params=params(16),
        name="sum_mix",
    )(zh, parts, pick, own)


def second_kernel(mixed_ref, trans_ref, out_ref):
    for z in range(0, 8, 2):
        rows = slice(z * 128, (z + 2) * 128)
        part = dot(trans_ref[0, rows], mixed_ref[:BLK])
        for i in range(1, trans_ref.shape[0]):
            part = part + dot(trans_ref[i, rows], mixed_ref[i * BLK : (i + 1) * BLK])
        for i in range(4):
            for s in range(2):
                out_ref[i % 2, s, z + i // 2] = part[i * 64 : (i + 1) * 64, s * 128 : (s + 1) * 128]


def multiply(mixed, trans):
    return pl.pallas_call(
        second_kernel,
        out_shape=shape((2, 2, 8, 64, 128), F32),
        in_specs=[WHOLE] * 2,
        out_specs=WHOLE,
        compiler_params=params(16),
        name="multiply",
    )(mixed, trans)


def last_kernel(parts_ref, keep_ref, out_ref):
    pieces = []
    for s in range(2):
        total = parts_ref[8 * s].astype(F32)
        for i in range(1, 8):
            total = total + parts_ref[8 * s + i].astype(F32)
        pieces.append(total)
    pieces.append(keep_ref[...].astype(F32))
    out_ref[...] = jnp.concatenate(pieces, 0).T.astype(BF).reshape(out_ref.shape)


def sum_and_join(parts, keep):
    _, cells, half = parts.shape
    return pl.pallas_call(
        last_kernel,
        out_shape=shape((half // 8, 8, 4 * cells)),
        compiler_params=params(16),
        name="sum_join",
    )(parts, keep)


def local(beta_last, transition, emission, successor, token_set):
    states, blocks, _, cells = beta_last.shape
    width = blocks * cells
    zh = jnp.full((1,), lax.axis_index("zh"), jnp.int32)
    plane = jnp.full((1,), lax.axis_index("y") * 4 + lax.axis_index("x"), jnp.int32)

    mine = as_rows(beta_last.reshape(states, blocks, cells))
    theirs = lax.ppermute(mine, "zh", [(0, 1), (1, 0)])
    beta = lax.all_to_all(pair_copies(zh, mine, theirs), PLANE, 0, 0).reshape(256, width)

    partial, pick, own, trans = mix_and_multiply(
        plane, beta, successor, token_set, emission.reshape(NSET, width), transition.reshape(width, -1)
    )
    near = near_sum(lax.all_to_all(partial, ("z0", "c"), 0, 0))
    parts = lax.all_to_all(near.reshape(8, cells, 256), ("zh", "z2", "z1"), 0, 0)
    copies, keep = sum_and_mix(zh, parts, pick, own)
    mixed = lax.all_to_all(copies, PLANE, 0, 0).reshape(width, 256)

    pair = lax.all_to_all(multiply(mixed, trans), "c", 0, 0)
    halves = (pair[0] + pair[1]).astype(BF).reshape(16, cells, 128)
    parts = lax.all_to_all(halves, ("zh", "z2", "z1", "z0"), 0, 0)
    moved = lax.all_to_all(sum_and_join(parts, keep), PLANE, 0, 0)
    moved = moved.reshape(16, states, 2, 2, cells).transpose(2, 1, 0, 3, 4)
    return moved.reshape(2, states, blocks, 1, cells)


def solution(mesh):
    fine = Mesh(mesh.devices.reshape(4, 4, 2, 2, 2, 2, 2), ("y", "x", "zh", "z2", "z1", "z0", "c"))
    dfa, hid = ("y", "x", "zh"), ("z2", "z1", "z0", "c")
    return jax.shard_map(
        local,
        mesh=fine,
        in_specs=(
            P(dfa, None, hid, None),
            P(None, hid, None, dfa),
            P(None, hid, None),
            P(),
            P(),
        ),
        out_specs=P(None, dfa, None, hid, None),
        check_vma=False,
    )
```

time: 714 us -> 157 us (0.22)
  the two profiles are of different devices: /device:TPU:2 before, /device:TPU:32 now
where the time goes in v2:
time: 157 us; the launch traced here: 156 us
  blocking collectives  101 us (64%)
  starting transfers between devices  21.9 us (14%)
  waiting for transfers between devices  16.9 us (11%)
  Pallas kernels  12.5 us (8%)
  local copies, waits for them, and re-layouts  4.3 us (3%)
    all_to_all x1, blocking collectives, local(): lax.all_to_all(near.reshape(8, cells, 256), ('zh', 'z2', 'z1'), 0, 0)  32.5 us
    all_to_all x1, blocking collectives, local(): parts = lax.all_to_all(halves, ('zh', 'z2', 'z1', 'z0'), 0, 0)  26.7 us
    all_to_all x1, blocking collectives, local(): mixed = lax.all_to_all(copies, PLANE, 0, 0).reshape(width, 256)  15.9 us
    ppermute x1, starting transfers between devices, local(): theirs = lax.ppermute(mine, 'zh', [(0, 1), (1, 0)])  14.8 us
    all_to_all x1, waiting for transfers between devices, local(): lax.all_to_all(pair_copies(zh, mine, theirs), PLANE, 0, 0)  14.6 us
    all_to_all x1, blocking collectives, local(): moved = lax.all_to_all(sum_and_join(parts, keep), PLANE, 0, 0)  10.6 us
    all_to_all x1, blocking collectives, local(): near = near_sum(lax.all_to_all(partial, ('z0', 'c'), 0, 0))  10.5 us
    pallas_call x1, Pallas kernels, mix_and_multiply(): pl.pallas_call(first_kernel, out_shape=(shape((4, outs // 4, states)), sh...  9.17 us
  transfers between devices with their start and end apart: 2, of which 2 were waited for; matrix products, arithmetic and copies ran while one was open for 1% of the time, Pallas kernels for 0%

profile of v2, /device:TPU:32, one launch (start us, length us, event | category | flops | bytes accessed | tf_op | source)
XLA Modules:
  0.0 156.5 jit_solution(6806754651927886711)
XLA Ops:
  0.0 0.0 copy-start.1
  0.0 0.8 copy-done.1
  0.8 0.1 as_rows.1.mine_ref
  1.0 14.8 %collective-permute-start = (bf16[8,2048]{1,0:T(8,128)(2,1)S(1)}, bf16[8,2048]{1,0:T(8,128)(2,1)S(1)}, u32[]{:S(2)}, u32[]{:S(2)}) collective-permute-start(bf16[8,2048]{1,0:T(8,128)(2,1)S(1)} %as_rows.1.mine_ref), channel_id=1, source_target_pairs={{0,16},{16,0},{1,17},{17,1},{2,18},{18,2},{3,19},{19,3},{4,20},{20... | collective-permute-start | bytes 98312 | tf_op jit(solution)/shard_map/ppermute | solution.py:232
  15.8 2.3 %collective-permute-done.theirs_ref = bf16[8,2048]{1,0:T(8,128)(2,1)S(1)} collective-permute-done((bf16[8,2048]{1,0:T(8,128)(2,1)S(1)}, bf16[8,2048]{1,0:T(8,128)(2,1)S(1)}, u32[]{:S(2)}, u32[]{:S(2)}) %collective-permute-start) | collective-permute-done | bytes 32800 | tf_op jit(solution)/shard_map/ppermute | solution.py:232
  18.1 1.1 pair_copies.1
  19.2 7.0 %all-to-all-start = ((bf16[16,16,2048]{2,1,0:T(8,128)(2,1)}), bf16[16,16,2048]{2,1,0:T(8,128)(2,1)S(1)}, u32[]{:S(2)}, u32[]{:S(2)}) async-start(bf16[16,16,2048]{2,1,0:T(8,128)(2,1)} %pair_copies.1), calls=%async_computation | async-start | bytes 2097152 | tf_op jit(solution)/shard_map/all_to_all | solution.py:233
  26.3 0.8 copy.6.succ_ref
  27.1 0.8 copy.7.sets_ref
  27.9 14.6 %all-to-all-done = bf16[16,16,2048]{2,1,0:T(8,128)(2,1)S(1)} async-done(((bf16[16,16,2048]{2,1,0:T(8,128)(2,1)}), bf16[16,16,2048]{2,1,0:T(8,128)(2,1)S(1)}, u32[]{:S(2)}, u32[]{:S(2)}) %all-to-all-start) | async-done | bytes 1048608 | tf_op jit(solution)/shard_map/all_to_all | solution.py:233
  42.5 0.0 copy-start
  42.5 0.9 copy-done
  43.4 9.2 %mix_multiply.1 = (bf16[4,256,256]{2,1,0:T(8,128)(2,1)S(1)}, bf16[2048,256]{1,0:T(8,128)(2,1)S(1)}, bf16[8,128,256]{2,1,0:T(8,128)(2,1)S(1)}, bf16[8,1024,256]{2,1,0:T(8,128)(2,1)S(1)}) custom-call(s32[1]{0:T(128)} %bitcast.1.plane_ref, bf16[256,2048]{1,0:T(8,128)(2,1)S(1)} %bitcast.11, s32[256,8]{1,0:T(8,128)S(1)} %copy.6.succ_ref, ...), custom_call_target="tpu_custom_call" | custom-call | tf_op jit(solution)/shard_map/mix_multiply/pallas_call | solution.py:107
  52.6 10.5 %all_to_all.35.parts_ref = bf16[4,256,256]{2,1,0:T(8,128)(2,1)S(1)} all-to-all(bf16[4,256,256]{2,1,0:T(8,128)(2,1)S(1)} %get-tuple-element.11), channel_id=1, replica_groups=mesh['y'=4,'x'=4,'zh'=2,'z2'=2,'z1'=2,'z0'=2,'c'=2] {'z0','c'}, dimensions={0} | all-to-all | bytes 1048576 | tf_op jit(solution)/shard_map/all_to_all | solution.py:238
  63.1 0.1 near_sum.1
  63.2 32.5 %all_to_all.36.parts_ref = bf16[8,64,256]{2,1,0:T(8,128)(2,1)S(1)} all-to-all(bf16[8,64,256]{2,1,0:T(8,128)(2,1)S(1)} %bitcast.13), channel_id=1, replica_groups=mesh['y'=4,'x'=4,'zh'=2,'z2'=2,'z1'=2,'z0'=2,'c'=2] {'zh','z2','z1'}, dimensions={0} | all-to-all | bytes 524288 | tf_op jit(solution)/shard_map/all_to_all | solution.py:239
  95.7 0.7 sum_mix.1
  96.4 15.9 %all_to_all.37 = bf16[16,128,256]{2,1,0:T(8,128)(2,1)S(1)} all-to-all(bf16[16,128,256]{2,1,0:T(8,128)(2,1)S(1)} %get-tuple-element.14), channel_id=1, replica_groups=mesh['y'=4,'x'=4,'zh'=2,'z2'=2,'z1'=2,'z0'=2,'c'=2] {'y','x'}, dimensions={0} | all-to-all | bytes 2097152 | tf_op jit(solution)/shard_map/all_to_all | solution.py:241
  112.3 1.2 multiply.1
  113.6 4.6 %all_to_all.38 = f32[2,2,8,64,128]{4,3,2,1,0:T(8,128)S(1)} all-to-all(f32[2,2,8,64,128]{4,3,2,1,0:T(8,128)S(1)} %multiply.1), channel_id=1, replica_groups=mesh['y'=4,'x'=4,'zh'=2,'z2'=2,'z1'=2,'z0'=2,'c'=2] {'c'}, dimensions={0} | all-to-all | bytes 2097152 | tf_op jit(solution)/shard_map/all_to_all | solution.py:243
  118.1 0.1 fusion
  118.2 26.7 %all_to_all.39.parts_ref = bf16[16,64,128]{2,1,0:T(8,128)(2,1)S(1)} all-to-all(bf16[16,64,128]{2,1,0:T(8,128)(2,1)S(1)} %bitcast.17), channel_id=1, replica_groups=mesh['y'=4,'x'=4,'zh'=2,'z2'=2,'z1'=2,'z0'=2,'c'=2] {'zh','z2','z1','z0'}, dimensions={0} | all-to-all | bytes 524288 | tf_op jit(solution)/shard_map/all_to_all | solution.py:245
  144.9 0.1 sum_join.1
  145.0 10.6 %all_to_all.40 = bf16[16,8,256]{2,1,0:T(8,128)(2,1)S(1)} all-to-all(bf16[16,8,256]{2,1,0:T(8,128)(2,1)S(1)} %sum_join.1), channel_id=1, replica_groups=mesh['y'=4,'x'=4,'zh'=2,'z2'=2,'z1'=2,'z0'=2,'c'=2] {'y','x'}, dimensions={0} | all-to-all | bytes 131072 | tf_op jit(solution)/shard_map/all_to_all | solution.py:246
  155.6 0.1 reshape.35
  155.7 0.8 copy.8
Async XLA Ops:
  0.0 0.8 copy-start.1
  1.0 17.2 %collective-permute-start = (bf16[8,2048]{1,0:T(8,128)(2,1)S(1)}, bf16[8,2048]{1,0:T(8,128)(2,1)S(1)}, u32[]{:S(2)}, u32[]{:S(2)}) collective-permute-start(bf16[8,2048]{1,0:T(8,128)(2,1)S(1)} %as_rows.1.mine_ref), channel_id=1, source_target_pairs={{0,16},{16,0},{1,17},{17,1},{2,18},{18,2},{3,19},{19,3},{4,20},{20... | collective-permute-start | bytes 98312 | tf_op jit(solution)/shard_map/ppermute | solution.py:232
  19.2 23.3 %all-to-all-start = ((bf16[16,16,2048]{2,1,0:T(8,128)(2,1)}), bf16[16,16,2048]{2,1,0:T(8,128)(2,1)S(1)}, u32[]{:S(2)}, u32[]{:S(2)}) async-start(bf16[16,16,2048]{2,1,0:T(8,128)(2,1)} %pair_copies.1), calls=%async_computation | async-start | bytes 2097152 | tf_op jit(solution)/shard_map/all_to_all | solution.py:233
  42.5 1.0 copy-start

commit v3 on v2

--- a/solution.py
+++ b/solution.py
@@ -46,54 +46,66 @@
     )(beta)
 
 
-def pair_kernel(zh_ref, mine_ref, theirs_ref, out_ref):
-    mine, theirs = mine_ref[...].astype(F32), theirs_ref[...].astype(F32)
-    first = zh_ref[0] == 0
-    both = jnp.concatenate([jnp.where(first, mine, theirs), jnp.where(first, theirs, mine)], 0).astype(BF)
+def copies_kernel(rows_ref, out_ref):
+    rows = rows_ref[...].astype(F32).reshape(out_ref.shape[1:]).astype(BF)
     for i in range(out_ref.shape[0]):
-        out_ref[i] = both
-
-
-def pair_copies(zh, mine, theirs):
-    states, width = mine.shape
-    return pl.pallas_call(
-        pair_kernel,
-        out_shape=shape((16, 2 * states, width)),
-        in_specs=[SCALAR, WHOLE, WHOLE],
-        compiler_params=params(16),
-        name="pair_copies",
-    )(zh, mine, theirs)
-
-
-def first_kernel(
-    plane_ref, beta_ref, succ_ref, sets_ref, emis_hbm, trans_hbm,
-    out_ref, pick_ref, own_ref, flip_ref,
-    emis_ref, trans, choose, total, arrived,
-):
-    emis_load = pltpu.make_async_copy(emis_hbm, emis_ref, arrived.at[0])
-    trans_load = pltpu.make_async_copy(trans_hbm, trans, arrived.at[1])
-    emis_load.start()
-    trans_load.start()
-    states, width = beta_ref.shape
+        out_ref[i] = rows
+
+
+def copies_of(rows):
+    _, states, width = rows.shape
+    return pl.pallas_call(
+        copies_kernel, out_shape=shape((16, 2 * states, width)), compiler_params=params(16), name="copies"
+    )(rows)
+
+
+def tables_kernel(place_ref, succ_ref, sets_ref, emis_ref, trans_ref, pick_ref, choose_ref, own_ref, flip_ref):
+    states = succ_ref.shape[0]
     lanes = own_ref.shape[1]
+    mine = emis_ref[:, pl.ds(pl.multiple_of(place_ref[0] * lanes, lanes), lanes)].astype(F32).T.astype(BF)
     for j in range(DEG):
         at = slice(j * states, (j + 1) * states)
         pick_ref[at] = (iota((states, states), 1) == succ_ref[:, j : j + 1]).astype(BF)
-        choose[at] = (iota((states, NSET), 1) == sets_ref[:, j : j + 1]).astype(BF)
-    emis_load.wait()
-    mine = emis_ref[:, pl.ds(pl.multiple_of(plane_ref[0] * lanes, lanes), lanes)].astype(F32).T.astype(BF)
-    for j in range(DEG):
-        own_ref[j] = dot(mine, choose[j * states : (j + 1) * states], ROWS).astype(BF)
+        choose = (iota((states, NSET), 1) == sets_ref[:, j : j + 1]).astype(BF)
+        choose_ref[at] = choose
+        own_ref[j] = dot(mine, choose, ROWS).astype(BF)
+    for b in range(flip_ref.shape[0]):
+        flip_ref[b] = trans_ref[b * BLK : (b + 1) * BLK].T
+
+
+def tables(place, succ, sets, emis, trans):
+    states = succ.shape[0]
+    width, outs = trans.shape
+    return pl.pallas_call(
+        tables_kernel,
+        out_shape=(
+            shape((DEG * states, states)),
+            shape((DEG * states, NSET)),
+            shape((DEG, 128, states)),
+            shape((width // BLK, outs, BLK)),
+        ),
+        in_specs=[SCALAR] + [WHOLE] * 4,
+        out_specs=(WHOLE,) * 4,
+        compiler_params=params(16),
+        cost_estimate=pl.CostEstimate(flops=2**31, bytes_accessed=12 * MIB, transcendentals=0),
+        name="tables",
+    )(place, succ, sets, emis, trans)
+
+
+def first_kernel(beta_ref, pick_ref, choose_ref, emis_ref, flip_hbm, out_ref, flip_ref, mixed_at, total, arrived):
+    load = pltpu.make_async_copy(flip_hbm, flip_ref, arrived)
+    load.start()
+    states, width = beta_ref.shape
     for b in range(width // BLK):
         cols = slice(b * BLK, (b + 1) * BLK)
         mixed = jnp.zeros((states, BLK), F32)
         for j in range(DEG):
             at = slice(j * states, (j + 1) * states)
-            mixed = mixed + dot(pick_ref[at], beta_ref[:, cols]) * dot(choose[at], emis_ref[:, cols])
-        if b == 0:
-            trans_load.wait()
-        flip_ref[b] = trans[cols].T
-        part = dot(flip_ref[b], mixed.astype(BF), ROWS)
+            mixed = mixed + dot(pick_ref[at], beta_ref[:, cols]) * dot(choose_ref[at], emis_ref[:, cols])
+        mixed_at[b] = mixed.astype(BF)
+    load.wait()
+    for b in range(width // BLK):
+        part = dot(flip_ref[b], mixed_at[b], ROWS)
         total[...] = part if b == 0 else total[...] + part
     for i in range(4):
         for z in range(4):
@@ -101,29 +113,22 @@
             out_ref[i, z * 64 : (z + 1) * 64] = total[at * 64 : (at + 1) * 64].astype(BF)
 
 
-def mix_and_multiply(plane, beta, succ, sets, emis, trans):
+def mix_and_multiply(beta, pick, choose, emis, flip):
     states = beta.shape[0]
-    width, outs = trans.shape
+    blocks, outs, _ = flip.shape
     return pl.pallas_call(
         first_kernel,
-        out_shape=(
-            shape((4, outs // 4, states)),
-            shape((DEG * states, states)),
-            shape((DEG, 128, states)),
-            shape((width // BLK, outs, BLK)),
-        ),
-        in_specs=[SCALAR] + [WHOLE] * 3 + [pl.BlockSpec(memory_space=pl.ANY)] * 2,
-        out_specs=(WHOLE,) * 4,
+        out_shape=(shape((4, outs // 4, states)), shape(flip.shape)),
+        in_specs=[WHOLE] * 4 + [pl.BlockSpec(memory_space=pl.ANY)],
+        out_specs=(WHOLE,) * 2,
         scratch_shapes=[
-            pltpu.VMEM((NSET, width), BF),
-            pltpu.VMEM((width, outs), BF),
-            pltpu.VMEM((DEG * states, NSET), BF),
+            pltpu.VMEM((blocks, states, BLK), BF),
             pltpu.VMEM((outs, states), F32),
-            pltpu.SemaphoreType.DMA((2,)),
+            pltpu.SemaphoreType.DMA(()),
         ],
         compiler_params=params(BIG),
         name="mix_multiply",
-    )(plane, beta, succ, sets, emis, trans)
+    )(beta, pick, choose, emis, flip)
 
 
 def near_kernel(parts_ref, out_ref):
@@ -145,7 +150,7 @@
     return (states >> 3 & 1) * 128 + (states >> 4) * 8 + (states & 7)
 
 
-def middle_kernel(zh_ref, parts_ref, pick_ref, own_ref, out_ref, keep_ref):
+def middle_kernel(place_ref, parts_ref, pick_ref, own_ref, out_ref, keep_ref):
     pieces = []
     for s in range(2):
         total = parts_ref[4 * s].astype(F32)
@@ -163,12 +168,12 @@
     for i in range(out_ref.shape[0]):
         out_ref[i] = mixed
     half = states // 2
-    place = half_place(iota((states, half), 0)) - zh_ref[0] * half
+    place = half_place(iota((states, half), 0)) - place_ref[1] * half
     mine = (iota((states, half), 1) == place).astype(BF)
     keep_ref[...] = dot(beta, mine).astype(BF)
 
 
-def sum_and_mix(zh, parts, pick, own):
+def sum_and_mix(place, parts, pick, own):
     _, cells, states = parts.shape
     return pl.pallas_call(
         middle_kernel,
@@ -176,7 +181,7 @@
         in_specs=[SCALAR, WHOLE, WHOLE, WHOLE],
         compiler_params=params(16),
         name="sum_mix",
-    )(zh, parts, pick, own)
+    )(place, parts, pick, own)
 
 
 def second_kernel(mixed_ref, trans_ref, out_ref):
@@ -225,19 +230,17 @@
 def local(beta_last, transition, emission, successor, token_set):
     states, blocks, _, cells = beta_last.shape
     width = blocks * cells
-    zh = jnp.full((1,), lax.axis_index("zh"), jnp.int32)
-    plane = jnp.full((1,), lax.axis_index("y") * 4 + lax.axis_index("x"), jnp.int32)
+    place = jnp.stack([lax.axis_index("y") * 4 + lax.axis_index("x"), lax.axis_index("zh")])
 
     mine = as_rows(beta_last.reshape(states, blocks, cells))
-    theirs = lax.ppermute(mine, "zh", [(0, 1), (1, 0)])
-    beta = lax.all_to_all(pair_copies(zh, mine, theirs), PLANE, 0, 0).reshape(256, width)
-
-    partial, pick, own, trans = mix_and_multiply(
-        plane, beta, successor, token_set, emission.reshape(NSET, width), transition.reshape(width, -1)
-    )
+    pair = lax.all_gather(mine, "zh", axis=0)
+    beta = lax.all_to_all(copies_of(pair), PLANE, 0, 0).reshape(256, width)
+    emis = emission.reshape(NSET, width)
+    pick, choose, own, flipped = tables(place, successor, token_set, emis, transition.reshape(width, -1))
+    partial, trans = mix_and_multiply(beta, pick, choose, emis, flipped)
     near = near_sum(lax.all_to_all(partial, ("z0", "c"), 0, 0))
     parts = lax.all_to_all(near.reshape(8, cells, 256), ("zh", "z2", "z1"), 0, 0)
-    copies, keep = sum_and_mix(zh, parts, pick, own)
+    copies, keep = sum_and_mix(place, parts, pick, own)
     mixed = lax.all_to_all(copies, PLANE, 0, 0).reshape(width, 256)
 
     pair = lax.all_to_all(multiply(mixed, trans), "c", 0, 0)

time: 157 us -> 152 us (0.968)
  blocking collectives: 101 us -> 117 us
  starting transfers between devices: 21.9 us -> 7.03 us
  waiting for transfers between devices: 16.9 us -> 5.46 us
  local copies, waits for them, and re-layouts: 4.3 us -> 10 us
    all_gather x0 -> x1, blocking collectives: none -> 15.9 us  [local(): pair = lax.all_gather(mine, 'zh', axis=0)]
    ppermute x1 -> x0, starting transfers between devices: 14.8 us -> none  [local(): theirs = lax.ppermute(mine, 'zh', [(0, 1), (1, 0)])]
    all_to_all x1, waiting for transfers between devices: 14.6 us -> 5.46 us  [local(): beta = lax.all_to_all(copies_of(pair), PLANE, 0, 0).reshape(256, width)]
    unnamed x6 -> x14, local copies, waits for them, and re-layouts: 3.43 us -> 9.18 us
    pallas_call x1, Pallas kernels: 9.17 us -> 5.83 us  [mix_and_multiply(): pl.pallas_call(first_kernel, out_shape=(shape((4, outs // 4, states)), sh...]
    ppermute x1 -> x0, waiting for transfers between devices: 2.32 us -> none  [local(): theirs = lax.ppermute(mine, 'zh', [(0, 1), (1, 0)])]
    pallas_call x1 -> x2, Pallas kernels: 1.08 us -> 3.37 us  [the longest x1 2.31 us: tables(): pl.pallas_call(tables_kernel, out_shape=(shape((DEG * states, states)), s...]
  transfers between devices with their start and end apart: 2 -> 1, of which waited for: 2 -> 1; matrix products, arithmetic and copies ran while one was open for 1% -> 2% of each run, Pallas kernels for 0% -> 2%
where the time goes in v3:
time: 152 us; the launch traced here: 151 us
  blocking collectives  117 us (77%)
  Pallas kernels  12 us (8%)
  local copies, waits for them, and re-layouts  10 us (7%)
  starting transfers between devices  7.03 us (5%)
  waiting for transfers between devices  5.46 us (4%)
    all_to_all x1, blocking collectives, local(): lax.all_to_all(near.reshape(8, cells, 256), ('zh', 'z2', 'z1'), 0, 0)  32.5 us
    all_to_all x1, blocking collectives, local(): parts = lax.all_to_all(halves, ('zh', 'z2', 'z1', 'z0'), 0, 0)  26.7 us
    all_to_all x1, blocking collectives, local(): mixed = lax.all_to_all(copies, PLANE, 0, 0).reshape(width, 256)  15.9 us
    all_gather x1, blocking collectives, local(): pair = lax.all_gather(mine, 'zh', axis=0)  15.9 us
    all_to_all x1, blocking collectives, local(): moved = lax.all_to_all(sum_and_join(parts, keep), PLANE, 0, 0)  10.6 us
    all_to_all x1, blocking collectives, local(): near = near_sum(lax.all_to_all(partial, ('z0', 'c'), 0, 0))  10.5 us
    unnamed x14, local copies, waits for them, and re-layouts  9.18 us
    all_to_all x1, starting transfers between devices, local(): beta = lax.all_to_all(copies_of(pair), PLANE, 0, 0).reshape(256, width)  7.03 us
  transfers between devices with their start and end apart: 1, of which 1 were waited for; matrix products, arithmetic and copies ran while one was open for 2% of the time, Pallas kernels for 2%

profile of v3, /device:TPU:32, one launch (start us, length us, event | category | flops | bytes accessed | tf_op | source)
XLA Modules:
  0.0 151.5 jit_solution(2439856419595917830)
XLA Ops:
  0.0 0.0 copy-start.4
  0.0 0.8 copy-done.4
  0.8 0.1 as_rows.1
  1.0 15.9 %all-gather = bf16[16,2048]{1,0:T(8,128)(2,1)S(1)} all-gather(bf16[8,2048]{1,0:T(8,128)(2,1)S(1)} %as_rows.1), channel_id=2, replica_groups=mesh['y'=4,'x'=4,'zh'=2,'z2'=2,'z1'=2,'z0'=2,'c'=2] {'zh'}, dimensions={0}, use_global_device_ids=true | all-gather | bytes 98304 | tf_op jit(solution)/shard_map/all_gather | solution.py:236
  16.9 1.1 copies.1
  17.9 7.0 %all-to-all-start = ((bf16[16,16,2048]{2,1,0:T(8,128)(2,1)}), bf16[16,16,2048]{2,1,0:T(8,128)(2,1)S(1)}, u32[]{:S(2)}, u32[]{:S(2)}) async-start(bf16[16,16,2048]{2,1,0:T(8,128)(2,1)} %copies.1), calls=%async_computation | async-start | bytes 2097152 | tf_op jit(solution)/shard_map/all_to_all | solution.py:237
  25.0 0.0 copy-start.2
  25.0 0.9 copy.6.succ_ref
  25.9 1.5 copy.7.sets_ref
  27.4 0.1 pad_add_fusion.place_ref
  27.4 0.0 copy-start.1
  27.4 0.9 copy-done.1
  28.4 0.0 copy-start.3
  28.4 0.9 copy-done.3
  29.3 0.0 copy-start.5
  29.3 2.2 %copy-done.5 = bf16[32,1,64,1024]{3,2,1,0:T(8,128)(2,1)S(1)} copy-done((bf16[32,1,64,1024]{3,2,1,0:T(8,128)(2,1)S(1)}, bf16[32,1,64,1024]{3,2,1,0:T(8,128)(2,1)}, u32[]{:S(2)}) %copy-start.5) | copy-done | bytes 4194328
  31.5 2.3 %tables.1 = (bf16[2048,256]{1,0:T(8,128)(2,1)S(1)}, bf16[2048,64]{1,0:T(8,128)(2,1)S(1)}, bf16[8,128,256]{2,1,0:T(8,128)(2,1)S(1)}, bf16[8,1024,256]{2,1,0:T(8,128)(2,1)S(1)}) custom-call(s32[2]{0:T(128)S(1)} %pad_add_fusion.place_ref, s32[256,8]{1,0:T(8,128)S(1)} %copy.6.succ_ref, s32[256,8]{1,0:T(8,128)S(1)} %copy-done.3, bf16[64,2048]{1,0:T(8,128)(2,1)S(1)} %bitcast.15, ...), custom_call_target="tpu_custom_call" | custom-call | flops 2147483648 | bytes 12582912 | tf_op jit(solution)/shard_map/tables/pallas_call | solution.py:79
  33.8 0.0 copy-start
  33.8 1.9 %copy-done = bf16[8,1024,256]{2,1,0:T(8,128)(2,1)} copy-done((bf16[8,1024,256]{2,1,0:T(8,128)(2,1)}, bf16[8,1024,256]{2,1,0:T(8,128)(2,1)S(1)}, u32[]{:S(2)}) %copy-start) | copy-done | bytes 4194328
  35.7 5.5 %all-to-all-done = bf16[16,16,2048]{2,1,0:T(8,128)(2,1)S(1)} async-done(((bf16[16,16,2048]{2,1,0:T(8,128)(2,1)}), bf16[16,16,2048]{2,1,0:T(8,128)(2,1)S(1)}, u32[]{:S(2)}, u32[]{:S(2)}) %all-to-all-start) | async-done | bytes 1048608 | tf_op jit(solution)/shard_map/all_to_all | solution.py:237
  41.2 0.0 copy-done.2
  41.2 5.8 %mix_multiply.1 = (bf16[4,256,256]{2,1,0:T(8,128)(2,1)S(1)}, bf16[8,1024,256]{2,1,0:T(8,128)(2,1)S(1)}) custom-call(bf16[256,2048]{1,0:T(8,128)(2,1)S(1)} %bitcast.12, bf16[2048,256]{1,0:T(8,128)(2,1)S(1)} %get-tuple-element.13.pick_ref, bf16[2048,64]{1,0:T(8,128)(2,1)S(1)} %get-tuple-element.14.choose_ref, bf16[64,2048]{1,0:T(8,128)(2,1)S(1)} %bitcast.16, ...), custom_call_target="tpu_custom_call" | custom-call | tf_op jit(solution)/shard_map/mix_multiply/pallas_call | solution.py:119
  47.0 10.5 %all_to_all.35.parts_ref = bf16[4,256,256]{2,1,0:T(8,128)(2,1)S(1)} all-to-all(bf16[4,256,256]{2,1,0:T(8,128)(2,1)S(1)} %get-tuple-element.16), channel_id=1, replica_groups=mesh['y'=4,'x'=4,'zh'=2,'z2'=2,'z1'=2,'z0'=2,'c'=2] {'z0','c'}, dimensions={0} | all-to-all | bytes 1048576 | tf_op jit(solution)/shard_map/all_to_all | solution.py:241
  57.6 0.1 near_sum.1
  57.6 32.5 %all_to_all.36.parts_ref = bf16[8,64,256]{2,1,0:T(8,128)(2,1)S(1)} all-to-all(bf16[8,64,256]{2,1,0:T(8,128)(2,1)S(1)} %bitcast.14), channel_id=1, replica_groups=mesh['y'=4,'x'=4,'zh'=2,'z2'=2,'z1'=2,'z0'=2,'c'=2] {'zh','z2','z1'}, dimensions={0} | all-to-all | bytes 524288 | tf_op jit(solution)/shard_map/all_to_all | solution.py:242
  90.1 1.2 sum_mix.1
  91.4 15.9 %all_to_all.37 = bf16[16,128,256]{2,1,0:T(8,128)(2,1)S(1)} all-to-all(bf16[16,128,256]{2,1,0:T(8,128)(2,1)S(1)} %get-tuple-element.18), channel_id=1, replica_groups=mesh['y'=4,'x'=4,'zh'=2,'z2'=2,'z1'=2,'z0'=2,'c'=2] {'y','x'}, dimensions={0} | all-to-all | bytes 2097152 | tf_op jit(solution)/shard_map/all_to_all | solution.py:244
  107.3 1.2 multiply.1
  108.5 4.6 %all_to_all.38 = f32[2,2,8,64,128]{4,3,2,1,0:T(8,128)S(1)} all-to-all(f32[2,2,8,64,128]{4,3,2,1,0:T(8,128)S(1)} %multiply.1), channel_id=1, replica_groups=mesh['y'=4,'x'=4,'zh'=2,'z2'=2,'z1'=2,'z0'=2,'c'=2] {'c'}, dimensions={0} | all-to-all | bytes 2097152 | tf_op jit(solution)/shard_map/all_to_all | solution.py:246
  113.1 0.1 fusion
  113.2 26.7 %all_to_all.39.parts_ref = bf16[16,64,128]{2,1,0:T(8,128)(2,1)S(1)} all-to-all(bf16[16,64,128]{2,1,0:T(8,128)(2,1)S(1)} %bitcast.20), channel_id=1, replica_groups=mesh['y'=4,'x'=4,'zh'=2,'z2'=2,'z1'=2,'z0'=2,'c'=2] {'zh','z2','z1','z0'}, dimensions={0} | all-to-all | bytes 524288 | tf_op jit(solution)/shard_map/all_to_all | solution.py:248
  139.9 0.1 sum_join.1
  140.0 10.6 %all_to_all.40 = bf16[16,8,256]{2,1,0:T(8,128)(2,1)S(1)} all-to-all(bf16[16,8,256]{2,1,0:T(8,128)(2,1)S(1)} %sum_join.1), channel_id=1, replica_groups=mesh['y'=4,'x'=4,'zh'=2,'z2'=2,'z1'=2,'z0'=2,'c'=2] {'y','x'}, dimensions={0} | all-to-all | bytes 131072 | tf_op jit(solution)/shard_map/all_to_all | solution.py:249
  150.6 0.1 reshape.35
  150.7 0.8 copy.8
Async XLA Ops:
  0.0 0.8 copy-start.4
  17.9 23.3 %all-to-all-start = ((bf16[16,16,2048]{2,1,0:T(8,128)(2,1)}), bf16[16,16,2048]{2,1,0:T(8,128)(2,1)S(1)}, u32[]{:S(2)}, u32[]{:S(2)}) async-start(bf16[16,16,2048]{2,1,0:T(8,128)(2,1)} %copies.1), calls=%async_computation | async-start | bytes 2097152 | tf_op jit(solution)/shard_map/all_to_all | solution.py:237
  25.0 16.2 %copy-start.2 = (bf16[64,1,2048]{2,0,1:T(8,128)(2,1)S(1)}, bf16[64,1,2048]{2,0,1:T(8,128)(2,1)}, u32[]{:S(2)}) copy-start(bf16[64,1,2048]{2,0,1:T(8,128)(2,1)} %param.7) | copy-start | bytes 786436
  27.4 0.9 copy-start.1
  28.4 0.9 copy-start.3
  29.3 2.2 %copy-start.5 = (bf16[32,1,64,1024]{3,2,1,0:T(8,128)(2,1)S(1)}, bf16[32,1,64,1024]{3,2,1,0:T(8,128)(2,1)}, u32[]{:S(2)}) copy-start(bf16[32,1,64,1024]{3,2,1,0:T(8,128)(2,1)} %param.6) | copy-start | bytes 12582916
  33.8 1.9 %copy-start = (bf16[8,1024,256]{2,1,0:T(8,128)(2,1)}, bf16[8,1024,256]{2,1,0:T(8,128)(2,1)S(1)}, u32[]{:S(2)}) copy-start(bf16[8,1024,256]{2,1,0:T(8,128)(2,1)S(1)} %get-tuple-element.15.flip_hbm) | copy-start | bytes 12582916

commit v4 on v3

--- a/solution.py
+++ b/solution.py
@@ -135,14 +135,15 @@
     total = parts_ref[0].astype(F32)
     for i in range(1, 4):
         total = total + parts_ref[i].astype(F32)
-    for i in range(2):
-        out_ref[i] = total.astype(BF)
+    cells = out_ref.shape[1]
+    for i in range(out_ref.shape[0]):
+        out_ref[i] = total[i // 2 * cells : (i // 2 + 1) * cells].astype(BF)
 
 
 def near_sum(parts):
     _, rows, states = parts.shape
     return pl.pallas_call(
-        near_kernel, out_shape=shape((2, rows, states)), compiler_params=params(16), name="near_sum"
+        near_kernel, out_shape=shape((8, rows // 4, states)), compiler_params=params(16), name="near_sum"
     )(parts)
 
 
@@ -153,9 +154,9 @@
 def middle_kernel(place_ref, parts_ref, pick_ref, own_ref, out_ref, keep_ref):
     pieces = []
     for s in range(2):
-        total = parts_ref[4 * s].astype(F32)
+        total = parts_ref[s].astype(F32)
         for i in range(1, 4):
-            total = total + parts_ref[4 * s + i].astype(F32)
+            total = total + parts_ref[2 * i + s].astype(F32)
         pieces.append(total)
     beta = jnp.concatenate(pieces, 0).astype(BF)
     states = beta.shape[1]
@@ -184,26 +185,30 @@
     )(place, parts, pick, own)
 
 
-def second_kernel(mixed_ref, trans_ref, out_ref):
-    for z in range(0, 8, 2):
-        rows = slice(z * 128, (z + 2) * 128)
+def second_kernel(place_ref, mixed_ref, trans_ref, keep_ref, send_ref):
+    first = place_ref[2] == 0
+    for z in range(4):
+        rows = slice(z * 256, (z + 1) * 256)
         part = dot(trans_ref[0, rows], mixed_ref[:BLK])
         for i in range(1, trans_ref.shape[0]):
             part = part + dot(trans_ref[i, rows], mixed_ref[i * BLK : (i + 1) * BLK])
-        for i in range(4):
+        for i in range(2):
             for s in range(2):
-                out_ref[i % 2, s, z + i // 2] = part[i * 64 : (i + 1) * 64, s * 128 : (s + 1) * 128]
-
-
-def multiply(mixed, trans):
+                lanes = slice(s * 128, (s + 1) * 128)
+                a, b = part[i * 128 : i * 128 + 64, lanes], part[i * 128 + 64 : (i + 1) * 128, lanes]
+                keep_ref[s * 8 + z * 2 + i] = jnp.where(first, a, b)
+                send_ref[s * 8 + z * 2 + i] = jnp.where(first, b, a).astype(BF)
+
+
+def multiply(place, mixed, trans):
     return pl.pallas_call(
         second_kernel,
-        out_shape=shape((2, 2, 8, 64, 128), F32),
-        in_specs=[WHOLE] * 2,
-        out_specs=WHOLE,
+        out_shape=(shape((16, 64, 128), F32), shape((16, 64, 128))),
+        in_specs=[SCALAR] + [WHOLE] * 2,
+        out_specs=(WHOLE,) * 2,
         compiler_params=params(16),
         name="multiply",
-    )(mixed, trans)
+    )(place, mixed, trans)
 
 
 def last_kernel(parts_ref, keep_ref, out_ref):
@@ -230,7 +235,8 @@
 def local(beta_last, transition, emission, successor, token_set):
     states, blocks, _, cells = beta_last.shape
     width = blocks * cells
-    place = jnp.stack([lax.axis_index("y") * 4 + lax.axis_index("x"), lax.axis_index("zh")])
+    plane = lax.axis_index("y") * 4 + lax.axis_index("x")
+    place = jnp.stack([plane, lax.axis_index("zh"), lax.axis_index("c")])
 
     mine = as_rows(beta_last.reshape(states, blocks, cells))
     pair = lax.all_gather(mine, "zh", axis=0)
@@ -239,12 +245,12 @@
     pick, choose, own, flipped = tables(place, successor, token_set, emis, transition.reshape(width, -1))
     partial, trans = mix_and_multiply(beta, pick, choose, emis, flipped)
     near = near_sum(lax.all_to_all(partial, ("z0", "c"), 0, 0))
-    parts = lax.all_to_all(near.reshape(8, cells, 256), ("zh", "z2", "z1"), 0, 0)
+    parts = lax.all_to_all(near, ("z2", "z1", "zh"), 0, 0)
     copies, keep = sum_and_mix(place, parts, pick, own)
     mixed = lax.all_to_all(copies, PLANE, 0, 0).reshape(width, 256)
 
-    pair = lax.all_to_all(multiply(mixed, trans), "c", 0, 0)
-    halves = (pair[0] + pair[1]).astype(BF).reshape(16, cells, 128)
+    kept, send = multiply(place, mixed, trans)
+    halves = (kept + lax.ppermute(send, "c", [(0, 1), (1, 0)]).astype(F32)).astype(BF)
     parts = lax.all_to_all(halves, ("zh", "z2", "z1", "z0"), 0, 0)
     moved = lax.all_to_all(sum_and_join(parts, keep), PLANE, 0, 0)
     moved = moved.reshape(16, states, 2, 2, cells).transpose(2, 1, 0, 3, 4)

time: 152 us -> 151 us (level)
  blocking collectives: 117 us -> 112 us
  starting transfers between devices: 7.03 us -> 8.96 us
    all_to_all x2 -> x1, blocking collectives: 37.1 us -> 29.5 us  [local(): parts = lax.all_to_all(near, ('z2', 'z1', 'zh'), 0, 0)]
    ppermute x0 -> x1, starting transfers between devices: none -> 1.92 us  [local(): lax.ppermute(send, 'c', [(0, 1), (1, 0)]).astype(F32)]
    all_to_all x1, blocking collectives: 26.7 us -> 28.3 us  [local(): parts = lax.all_to_all(halves, ('zh', 'z2', 'z1', 'z0'), 0, 0)]
  transfers between devices with their start and end apart: 1 -> 2, of which waited for: 1 -> 2; matrix products, arithmetic and copies ran while one was open for 2% -> 2% of each run, Pallas kernels for 2% -> 2%
where the time goes in v4:
time: 151 us
  blocking collectives  112 us (74%)
  Pallas kernels  12.5 us (8%)
  local copies, waits for them, and re-layouts  10 us (7%)
  starting transfers between devices  8.96 us (6%)
  waiting for transfers between devices  6.96 us (5%)
    all_to_all x1, blocking collectives, local(): parts = lax.all_to_all(near, ('z2', 'z1', 'zh'), 0, 0)  29.5 us
    all_to_all x1, blocking collectives, local(): parts = lax.all_to_all(halves, ('zh', 'z2', 'z1', 'z0'), 0, 0)  28.3 us
    all_to_all x1, blocking collectives, local(): mixed = lax.all_to_all(copies, PLANE, 0, 0).reshape(width, 256)  17.2 us
    all_gather x1, blocking collectives, local(): pair = lax.all_gather(mine, 'zh', axis=0)  15.9 us
    all_to_all x1, blocking collectives, local(): moved = lax.all_to_all(sum_and_join(parts, keep), PLANE, 0, 0)  10.6 us
    all_to_all x1, blocking collectives, local(): near = near_sum(lax.all_to_all(partial, ('z0', 'c'), 0, 0))  10.5 us
    unnamed x14, local copies, waits for them, and re-layouts  9.18 us
    all_to_all x1, starting transfers between devices, local(): beta = lax.all_to_all(copies_of(pair), PLANE, 0, 0).reshape(256, width)  7.03 us
  transfers between devices with their start and end apart: 2, of which 2 were waited for; matrix products, arithmetic and copies ran while one was open for 2% of the time, Pallas kernels for 2%

profile of v4, /device:TPU:32, one launch (start us, length us, event | category | flops | bytes accessed | tf_op | source)
XLA Modules:
  0.0 150.8 jit_solution(1922298382457774176)
XLA Ops:
  0.0 0.0 copy-start.4
  0.0 0.8 copy-done.4
  0.8 0.1 as_rows.1
  1.0 15.9 %all-gather = bf16[16,2048]{1,0:T(8,128)(2,1)S(1)} all-gather(bf16[8,2048]{1,0:T(8,128)(2,1)S(1)} %as_rows.1), channel_id=2, replica_groups=mesh['y'=4,'x'=4,'zh'=2,'z2'=2,'z1'=2,'z0'=2,'c'=2] {'zh'}, dimensions={0}, use_global_device_ids=true | all-gather | bytes 98304 | tf_op jit(solution)/shard_map/all_gather | solution.py:242
  16.9 1.1 copies.1
  17.9 7.0 %all-to-all-start = ((bf16[16,16,2048]{2,1,0:T(8,128)(2,1)}), bf16[16,16,2048]{2,1,0:T(8,128)(2,1)S(1)}, u32[]{:S(2)}, u32[]{:S(2)}) async-start(bf16[16,16,2048]{2,1,0:T(8,128)(2,1)} %copies.1), calls=%async_computation | async-start | bytes 2097152 | tf_op jit(solution)/shard_map/all_to_all | solution.py:243
  25.0 0.0 copy-start.2
  25.0 0.9 copy.6.succ_ref
  25.9 1.5 copy.7.sets_ref
  27.4 0.1 pad_add_fusion.place_ref
  27.4 0.0 copy-start.1
  27.4 0.9 copy-done.1
  28.4 0.0 copy-start.3
  28.4 0.9 copy-done.3
  29.3 0.0 copy-start.5
  29.3 2.2 %copy-done.5 = bf16[32,1,64,1024]{3,2,1,0:T(8,128)(2,1)S(1)} copy-done((bf16[32,1,64,1024]{3,2,1,0:T(8,128)(2,1)S(1)}, bf16[32,1,64,1024]{3,2,1,0:T(8,128)(2,1)}, u32[]{:S(2)}) %copy-start.5) | copy-done | bytes 4194328
  31.5 2.3 %tables.1 = (bf16[2048,256]{1,0:T(8,128)(2,1)S(1)}, bf16[2048,64]{1,0:T(8,128)(2,1)S(1)}, bf16[8,128,256]{2,1,0:T(8,128)(2,1)S(1)}, bf16[8,1024,256]{2,1,0:T(8,128)(2,1)S(1)}) custom-call(s32[3]{0:T(128)S(1)} %pad_add_fusion.place_ref, s32[256,8]{1,0:T(8,128)S(1)} %copy.6.succ_ref, s32[256,8]{1,0:T(8,128)S(1)} %copy-done.3, bf16[64,2048]{1,0:T(8,128)(2,1)S(1)} %bitcast.13, ...), custom_call_target="tpu_custom_call" | custom-call | flops 2147483648 | bytes 12582912 | tf_op jit(solution)/shard_map/tables/pallas_call | solution.py:79
  33.8 0.0 copy-start
  33.8 1.9 %copy-done = bf16[8,1024,256]{2,1,0:T(8,128)(2,1)} copy-done((bf16[8,1024,256]{2,1,0:T(8,128)(2,1)}, bf16[8,1024,256]{2,1,0:T(8,128)(2,1)S(1)}, u32[]{:S(2)}) %copy-start) | copy-done | bytes 4194328
  35.7 5.5 %all-to-all-done = bf16[16,16,2048]{2,1,0:T(8,128)(2,1)S(1)} async-done(((bf16[16,16,2048]{2,1,0:T(8,128)(2,1)}), bf16[16,16,2048]{2,1,0:T(8,128)(2,1)S(1)}, u32[]{:S(2)}, u32[]{:S(2)}) %all-to-all-start) | async-done | bytes 1048608 | tf_op jit(solution)/shard_map/all_to_all | solution.py:243
  41.2 0.0 copy-done.2
  41.2 5.8 %mix_multiply.1 = (bf16[4,256,256]{2,1,0:T(8,128)(2,1)S(1)}, bf16[8,1024,256]{2,1,0:T(8,128)(2,1)S(1)}) custom-call(bf16[256,2048]{1,0:T(8,128)(2,1)S(1)} %bitcast.11, bf16[2048,256]{1,0:T(8,128)(2,1)S(1)} %get-tuple-element.15.pick_ref, bf16[2048,64]{1,0:T(8,128)(2,1)S(1)} %get-tuple-element.16.choose_ref, bf16[64,2048]{1,0:T(8,128)(2,1)S(1)} %bitcast.14, ...), custom_call_target="tpu_custom_call" | custom-call | tf_op jit(solution)/shard_map/mix_multiply/pallas_call | solution.py:119
  47.1 10.5 %all_to_all.30.parts_ref = bf16[4,256,256]{2,1,0:T(8,128)(2,1)S(1)} all-to-all(bf16[4,256,256]{2,1,0:T(8,128)(2,1)S(1)} %get-tuple-element.18), channel_id=1, replica_groups=mesh['y'=4,'x'=4,'zh'=2,'z2'=2,'z1'=2,'z0'=2,'c'=2] {'z0','c'}, dimensions={0} | all-to-all | bytes 1048576 | tf_op jit(solution)/shard_map/all_to_all | solution.py:247
  57.6 0.1 near_sum.1
  57.6 29.5 %all_to_all.31.parts_ref = bf16[8,64,256]{2,1,0:T(8,128)(2,1)S(1)} all-to-all(bf16[8,64,256]{2,1,0:T(8,128)(2,1)S(1)} %near_sum.1), channel_id=1, replica_groups=mesh['y'=4,'x'=4,'zh'=2,'z2'=2,'z1'=2,'z0'=2,'c'=2] {'z2','z1','zh'}, dimensions={0} | all-to-all | bytes 524288 | tf_op jit(solution)/shard_map/all_to_all | solution.py:248
  87.1 1.2 sum_mix.1
  88.4 17.2 %all_to_all.32 = bf16[16,128,256]{2,1,0:T(8,128)(2,1)S(1)} all-to-all(bf16[16,128,256]{2,1,0:T(8,128)(2,1)S(1)} %get-tuple-element.20), channel_id=1, replica_groups=mesh['y'=4,'x'=4,'zh'=2,'z2'=2,'z1'=2,'z0'=2,'c'=2] {'y','x'}, dimensions={0} | all-to-all | bytes 2097152 | tf_op jit(solution)/shard_map/all_to_all | solution.py:250
  105.6 1.8 %multiply.1 = (f32[16,64,128]{2,1,0:T(8,128)S(1)}, bf16[16,64,128]{2,1,0:T(8,128)(2,1)S(1)}) custom-call(s32[3]{0:T(128)S(1)} %pad_add_fusion.place_ref, bf16[2048,256]{1,0:T(8,128)(2,1)S(1)} %bitcast.12, bf16[8,1024,256]{2,1,0:T(8,128)(2,1)S(1)} %get-tuple-element.21.trans_ref), custom_call_target="tpu_custom_call" | custom-call | tf_op jit(solution)/shard_map/multiply/pallas_call | solution.py:204
  107.4 1.9 %collective-permute-start = (bf16[16,64,128]{2,1,0:T(8,128)(2,1)S(1)}, bf16[16,64,128]{2,1,0:T(8,128)(2,1)S(1)}, u32[]{:S(2)}, u32[]{:S(2)}) collective-permute-start(bf16[16,64,128]{2,1,0:T(8,128)(2,1)S(1)} %get-tuple-element.23), channel_id=1, source_target_pairs={{0,1},{1,0},{2,3},{3,2},{4,5},{5,4},{6,7},{7,6},{8,9},{9,8},{10,11... | collective-permute-start | bytes 786440 | tf_op jit(solution)/shard_map/ppermute | solution.py:253
  109.3 1.5 collective-permute-done
  110.8 0.1 add_convert_fusion
  110.9 28.3 %all_to_all.33.parts_ref = bf16[16,64,128]{2,1,0:T(8,128)(2,1)S(1)} all-to-all(bf16[16,64,128]{2,1,0:T(8,128)(2,1)S(1)} %add_convert_fusion), channel_id=1, replica_groups=mesh['y'=4,'x'=4,'zh'=2,'z2'=2,'z1'=2,'z0'=2,'c'=2] {'zh','z2','z1','z0'}, dimensions={0} | all-to-all | bytes 524288 | tf_op jit(solution)/shard_map/all_to_all | solution.py:254
  139.2 0.1 sum_join.1
  139.3 10.6 %all_to_all.34 = bf16[16,8,256]{2,1,0:T(8,128)(2,1)S(1)} all-to-all(bf16[16,8,256]{2,1,0:T(8,128)(2,1)S(1)} %sum_join.1), channel_id=1, replica_groups=mesh['y'=4,'x'=4,'zh'=2,'z2'=2,'z1'=2,'z0'=2,'c'=2] {'y','x'}, dimensions={0} | all-to-all | bytes 131072 | tf_op jit(solution)/shard_map/all_to_all | solution.py:255
  150.0 0.1 reshape.26
  150.1 0.8 copy.8
Async XLA Ops:
  0.0 0.8 copy-start.4
  17.9 23.3 %all-to-all-start = ((bf16[16,16,2048]{2,1,0:T(8,128)(2,1)}), bf16[16,16,2048]{2,1,0:T(8,128)(2,1)S(1)}, u32[]{:S(2)}, u32[]{:S(2)}) async-start(bf16[16,16,2048]{2,1,0:T(8,128)(2,1)} %copies.1), calls=%async_computation | async-start | bytes 2097152 | tf_op jit(solution)/shard_map/all_to_all | solution.py:243
  25.0 16.2 %copy-start.2 = (bf16[64,1,2048]{2,0,1:T(8,128)(2,1)S(1)}, bf16[64,1,2048]{2,0,1:T(8,128)(2,1)}, u32[]{:S(2)}) copy-start(bf16[64,1,2048]{2,0,1:T(8,128)(2,1)} %param.7) | copy-start | bytes 786436
  27.4 1.0 copy-start.1
  28.4 0.9 copy-start.3
  29.3 2.2 %copy-start.5 = (bf16[32,1,64,1024]{3,2,1,0:T(8,128)(2,1)S(1)}, bf16[32,1,64,1024]{3,2,1,0:T(8,128)(2,1)}, u32[]{:S(2)}) copy-start(bf16[32,1,64,1024]{3,2,1,0:T(8,128)(2,1)} %param.6) | copy-start | bytes 12582916
  33.8 2.0 %copy-start = (bf16[8,1024,256]{2,1,0:T(8,128)(2,1)}, bf16[8,1024,256]{2,1,0:T(8,128)(2,1)S(1)}, u32[]{:S(2)}) copy-start(bf16[8,1024,256]{2,1,0:T(8,128)(2,1)S(1)} %get-tuple-element.17.flip_hbm) | copy-start | bytes 12582916
  107.4 3.4 %collective-permute-start = (bf16[16,64,128]{2,1,0:T(8,128)(2,1)S(1)}, bf16[16,64,128]{2,1,0:T(8,128)(2,1)S(1)}, u32[]{:S(2)}, u32[]{:S(2)}) collective-permute-start(bf16[16,64,128]{2,1,0:T(8,128)(2,1)S(1)} %get-tuple-element.23), channel_id=1, source_target_pairs={{0,1},{1,0},{2,3},{3,2},{4,5},{5,4},{6,7},{7,6},{8,9},{9,8},{10,11... | collective-permute-start | bytes 786440 | tf_op jit(solution)/shard_map/ppermute | solution.py:253

commit v5 on v4

--- a/solution.py
+++ b/solution.py
@@ -151,7 +151,7 @@
     return (states >> 3 & 1) * 128 + (states >> 4) * 8 + (states & 7)
 
 
-def middle_kernel(place_ref, parts_ref, pick_ref, own_ref, out_ref, keep_ref):
+def middle_kernel(parts_ref, pick_ref, own_ref, out_ref, keep_ref):
     pieces = []
     for s in range(2):
         total = parts_ref[s].astype(F32)
@@ -169,24 +169,24 @@
     for i in range(out_ref.shape[0]):
         out_ref[i] = mixed
     half = states // 2
-    place = half_place(iota((states, half), 0)) - place_ref[1] * half
+    place = half_place(iota((states, half), 0)) - lax.axis_index("zh") * half
     mine = (iota((states, half), 1) == place).astype(BF)
     keep_ref[...] = dot(beta, mine).astype(BF)
 
 
-def sum_and_mix(place, parts, pick, own):
+def sum_and_mix(parts, pick, own):
     _, cells, states = parts.shape
     return pl.pallas_call(
         middle_kernel,
         out_shape=(shape((16, 2 * cells, states)), shape((2 * cells, states // 2))),
-        in_specs=[SCALAR, WHOLE, WHOLE, WHOLE],
+        in_specs=[WHOLE] * 3,
         compiler_params=params(16),
         name="sum_mix",
-    )(place, parts, pick, own)
-
-
-def second_kernel(place_ref, mixed_ref, trans_ref, keep_ref, send_ref):
-    first = place_ref[2] == 0
+    )(parts, pick, own)
+
+
+def second_kernel(mixed_ref, trans_ref, keep_ref, send_ref):
+    first = lax.axis_index("c") == 0
     for z in range(4):
         rows = slice(z * 256, (z + 1) * 256)
         part = dot(trans_ref[0, rows], mixed_ref[:BLK])
@@ -200,15 +200,15 @@
                 send_ref[s * 8 + z * 2 + i] = jnp.where(first, b, a).astype(BF)
 
 
-def multiply(place, mixed, trans):
+def multiply(mixed, trans):
     return pl.pallas_call(
         second_kernel,
         out_shape=(shape((16, 64, 128), F32), shape((16, 64, 128))),
-        in_specs=[SCALAR] + [WHOLE] * 2,
+        in_specs=[WHOLE] * 2,
         out_specs=(WHOLE,) * 2,
         compiler_params=params(16),
         name="multiply",
-    )(place, mixed, trans)
+    )(mixed, trans)
 
 
 def last_kernel(parts_ref, keep_ref, out_ref):
@@ -236,7 +236,7 @@
     states, blocks, _, cells = beta_last.shape
     width = blocks * cells
     plane = lax.axis_index("y") * 4 + lax.axis_index("x")
-    place = jnp.stack([plane, lax.axis_index("zh"), lax.axis_index("c")])
+    place = jnp.full((1,), plane, jnp.int32)
 
     mine = as_rows(beta_last.reshape(states, blocks, cells))
     pair = lax.all_gather(mine, "zh", axis=0)
@@ -246,10 +246,10 @@
     partial, trans = mix_and_multiply(beta, pick, choose, emis, flipped)
     near = near_sum(lax.all_to_all(partial, ("z0", "c"), 0, 0))
     parts = lax.all_to_all(near, ("z2", "z1", "zh"), 0, 0)
-    copies, keep = sum_and_mix(place, parts, pick, own)
+    copies, keep = sum_and_mix(parts, pick, own)
     mixed = lax.all_to_all(copies, PLANE, 0, 0).reshape(width, 256)
 
-    kept, send = multiply(place, mixed, trans)
+    kept, send = multiply(mixed, trans)
     halves = (kept + lax.ppermute(send, "c", [(0, 1), (1, 0)]).astype(F32)).astype(BF)
     parts = lax.all_to_all(halves, ("zh", "z2", "z1", "z0"), 0, 0)
     moved = lax.all_to_all(sum_and_join(parts, keep), PLANE, 0, 0)

time: 151 us -> 150 us (level)
  Pallas kernels: 12.5 us -> 10.9 us
  transfers between devices with their start and end apart: 2 -> 2, of which waited for: 2 -> 2; matrix products, arithmetic and copies ran while one was open for 2% -> 2% of each run, Pallas kernels for 2% -> 1%
where the time goes in v5:
time: 150 us
  blocking collectives  112 us (75%)
  Pallas kernels  10.9 us (7%)
  local copies, waits for them, and re-layouts  10 us (7%)
  starting transfers between devices  8.96 us (6%)
  waiting for transfers between devices  7.57 us (5%)
    all_to_all x1, blocking collectives, local(): parts = lax.all_to_all(near, ('z2', 'z1', 'zh'), 0, 0)  29.5 us
    all_to_all x1, blocking collectives, local(): parts = lax.all_to_all(halves, ('zh', 'z2', 'z1', 'z0'), 0, 0)  28.3 us
    all_to_all x1, blocking collectives, local(): mixed = lax.all_to_all(copies, PLANE, 0, 0).reshape(width, 256)  17.2 us
    all_gather x1, blocking collectives, local(): pair = lax.all_gather(mine, 'zh', axis=0)  15.9 us
    all_to_all x1, blocking collectives, local(): moved = lax.all_to_all(sum_and_join(parts, keep), PLANE, 0, 0)  10.6 us
    all_to_all x1, blocking collectives, local(): near = near_sum(lax.all_to_all(partial, ('z0', 'c'), 0, 0))  10.5 us
    unnamed x14, local copies, waits for them, and re-layouts  9.18 us
    all_to_all x1, starting transfers between devices, local(): beta = lax.all_to_all(copies_of(pair), PLANE, 0, 0).reshape(256, width)  7.03 us
  transfers between devices with their start and end apart: 2, of which 2 were waited for; matrix products, arithmetic and copies ran while one was open for 2% of the time, Pallas kernels for 1%

profile of v5, /device:TPU:32, one launch (start us, length us, event | category | flops | bytes accessed | tf_op | source)
XLA Modules:
  0.0 149.7 jit_solution(17108161283560932950)
XLA Ops:
  0.0 0.0 copy-start.4
  0.0 0.8 copy-done.4
  0.8 0.1 as_rows.1
  1.0 15.9 %all-gather = bf16[16,2048]{1,0:T(8,128)(2,1)S(1)} all-gather(bf16[8,2048]{1,0:T(8,128)(2,1)S(1)} %as_rows.1), channel_id=2, replica_groups=mesh['y'=4,'x'=4,'zh'=2,'z2'=2,'z1'=2,'z0'=2,'c'=2] {'zh'}, dimensions={0}, use_global_device_ids=true | all-gather | bytes 98304 | tf_op jit(solution)/shard_map/all_gather | solution.py:242
  16.9 1.1 copies.1
  17.9 7.0 %all-to-all-start = ((bf16[16,16,2048]{2,1,0:T(8,128)(2,1)}), bf16[16,16,2048]{2,1,0:T(8,128)(2,1)S(1)}, u32[]{:S(2)}, u32[]{:S(2)}) async-start(bf16[16,16,2048]{2,1,0:T(8,128)(2,1)} %copies.1), calls=%async_computation | async-start | bytes 2097152 | tf_op jit(solution)/shard_map/all_to_all | solution.py:243
  25.0 0.0 copy-start.2
  25.0 0.9 copy.6.succ_ref
  25.9 1.5 copy.7.sets_ref
  27.4 0.0 copy-start.1
  27.4 0.9 copy-done.1
  28.3 0.0 copy-start.3
  28.3 0.9 copy-done.3
  29.2 0.0 copy-start.5
  29.2 2.2 %copy-done.5 = bf16[32,1,64,1024]{3,2,1,0:T(8,128)(2,1)S(1)} copy-done((bf16[32,1,64,1024]{3,2,1,0:T(8,128)(2,1)S(1)}, bf16[32,1,64,1024]{3,2,1,0:T(8,128)(2,1)}, u32[]{:S(2)}) %copy-start.5) | copy-done | bytes 4194328
  31.4 1.8 %tables.1 = (bf16[2048,256]{1,0:T(8,128)(2,1)S(1)}, bf16[2048,64]{1,0:T(8,128)(2,1)S(1)}, bf16[8,128,256]{2,1,0:T(8,128)(2,1)S(1)}, bf16[8,1024,256]{2,1,0:T(8,128)(2,1)S(1)}) custom-call(s32[1]{0:T(128)} %bitcast.3.place_ref, s32[256,8]{1,0:T(8,128)S(1)} %copy.6.succ_ref, s32[256,8]{1,0:T(8,128)S(1)} %copy-done.3, bf16[64,2048]{1,0:T(8,128)(2,1)S(1)} %bitcast.11, ...), custom_call_target="tpu_custom_call" | custom-call | flops 2147483648 | bytes 12582912 | tf_op jit(solution)/shard_map/tables/pallas_call | solution.py:79
  33.2 0.0 copy-start
  33.2 1.9 %copy-done = bf16[8,1024,256]{2,1,0:T(8,128)(2,1)} copy-done((bf16[8,1024,256]{2,1,0:T(8,128)(2,1)}, bf16[8,1024,256]{2,1,0:T(8,128)(2,1)S(1)}, u32[]{:S(2)}) %copy-start) | copy-done | bytes 4194328
  35.1 6.1 %all-to-all-done = bf16[16,16,2048]{2,1,0:T(8,128)(2,1)S(1)} async-done(((bf16[16,16,2048]{2,1,0:T(8,128)(2,1)}), bf16[16,16,2048]{2,1,0:T(8,128)(2,1)S(1)}, u32[]{:S(2)}, u32[]{:S(2)}) %all-to-all-start) | async-done | bytes 1048608 | tf_op jit(solution)/shard_map/all_to_all | solution.py:243
  41.2 0.0 copy-done.2
  41.2 5.8 %mix_multiply.1 = (bf16[4,256,256]{2,1,0:T(8,128)(2,1)S(1)}, bf16[8,1024,256]{2,1,0:T(8,128)(2,1)S(1)}) custom-call(bf16[256,2048]{1,0:T(8,128)(2,1)S(1)} %bitcast.9, bf16[2048,256]{1,0:T(8,128)(2,1)S(1)} %get-tuple-element.15.pick_ref, bf16[2048,64]{1,0:T(8,128)(2,1)S(1)} %get-tuple-element.16.choose_ref, bf16[64,2048]{1,0:T(8,128)(2,1)S(1)} %bitcast.12, ...), custom_call_target="tpu_custom_call" | custom-call | tf_op jit(solution)/shard_map/mix_multiply/pallas_call | solution.py:119
  47.1 10.5 %all_to_all.30.parts_ref = bf16[4,256,256]{2,1,0:T(8,128)(2,1)S(1)} all-to-all(bf16[4,256,256]{2,1,0:T(8,128)(2,1)S(1)} %get-tuple-element.18), channel_id=1, replica_groups=mesh['y'=4,'x'=4,'zh'=2,'z2'=2,'z1'=2,'z0'=2,'c'=2] {'z0','c'}, dimensions={0} | all-to-all | bytes 1048576 | tf_op jit(solution)/shard_map/all_to_all | solution.py:247
  57.6 0.1 near_sum.1
  57.6 29.5 %all_to_all.31.parts_ref = bf16[8,64,256]{2,1,0:T(8,128)(2,1)S(1)} all-to-all(bf16[8,64,256]{2,1,0:T(8,128)(2,1)S(1)} %near_sum.1), channel_id=1, replica_groups=mesh['y'=4,'x'=4,'zh'=2,'z2'=2,'z1'=2,'z0'=2,'c'=2] {'z2','z1','zh'}, dimensions={0} | all-to-all | bytes 524288 | tf_op jit(solution)/shard_map/all_to_all | solution.py:248
  87.1 0.7 sum_mix.1
  87.8 17.2 %all_to_all.32 = bf16[16,128,256]{2,1,0:T(8,128)(2,1)S(1)} all-to-all(bf16[16,128,256]{2,1,0:T(8,128)(2,1)S(1)} %get-tuple-element.20), channel_id=1, replica_groups=mesh['y'=4,'x'=4,'zh'=2,'z2'=2,'z1'=2,'z0'=2,'c'=2] {'y','x'}, dimensions={0} | all-to-all | bytes 2097152 | tf_op jit(solution)/shard_map/all_to_all | solution.py:250
  105.0 1.2 multiply.1
  106.3 1.9 %collective-permute-start = (bf16[16,64,128]{2,1,0:T(8,128)(2,1)S(1)}, bf16[16,64,128]{2,1,0:T(8,128)(2,1)S(1)}, u32[]{:S(2)}, u32[]{:S(2)}) collective-permute-start(bf16[16,64,128]{2,1,0:T(8,128)(2,1)S(1)} %get-tuple-element.23), channel_id=1, source_target_pairs={{0,1},{1,0},{2,3},{3,2},{4,5},{5,4},{6,7},{7,6},{8,9},{9,8},{10,11... | collective-permute-start | bytes 786440 | tf_op jit(solution)/shard_map/ppermute | solution.py:253
  108.2 1.5 %collective-permute-done = bf16[16,64,128]{2,1,0:T(8,128)(2,1)S(1)} collective-permute-done((bf16[16,64,128]{2,1,0:T(8,128)(2,1)S(1)}, bf16[16,64,128]{2,1,0:T(8,128)(2,1)S(1)}, u32[]{:S(2)}, u32[]{:S(2)}) %collective-permute-start) | collective-permute-done | bytes 262176 | tf_op jit(solution)/shard_map/ppermute | solution.py:253
  109.7 0.1 add_convert_fusion
  109.8 28.3 %all_to_all.33.parts_ref = bf16[16,64,128]{2,1,0:T(8,128)(2,1)S(1)} all-to-all(bf16[16,64,128]{2,1,0:T(8,128)(2,1)S(1)} %add_convert_fusion), channel_id=1, replica_groups=mesh['y'=4,'x'=4,'zh'=2,'z2'=2,'z1'=2,'z0'=2,'c'=2] {'zh','z2','z1','z0'}, dimensions={0} | all-to-all | bytes 524288 | tf_op jit(solution)/shard_map/all_to_all | solution.py:254
  138.1 0.1 sum_join.1
  138.2 10.6 %all_to_all.34 = bf16[16,8,256]{2,1,0:T(8,128)(2,1)S(1)} all-to-all(bf16[16,8,256]{2,1,0:T(8,128)(2,1)S(1)} %sum_join.1), channel_id=1, replica_groups=mesh['y'=4,'x'=4,'zh'=2,'z2'=2,'z1'=2,'z0'=2,'c'=2] {'y','x'}, dimensions={0} | all-to-all | bytes 131072 | tf_op jit(solution)/shard_map/all_to_all | solution.py:255
  148.9 0.1 reshape.26
  149.0 0.8 copy.8
Async XLA Ops:
  0.0 0.8 copy-start.4
  17.9 23.3 %all-to-all-start = ((bf16[16,16,2048]{2,1,0:T(8,128)(2,1)}), bf16[16,16,2048]{2,1,0:T(8,128)(2,1)S(1)}, u32[]{:S(2)}, u32[]{:S(2)}) async-start(bf16[16,16,2048]{2,1,0:T(8,128)(2,1)} %copies.1), calls=%async_computation | async-start | bytes 2097152 | tf_op jit(solution)/shard_map/all_to_all | solution.py:243
  25.0 16.2 %copy-start.2 = (bf16[64,1,2048]{2,0,1:T(8,128)(2,1)S(1)}, bf16[64,1,2048]{2,0,1:T(8,128)(2,1)}, u32[]{:S(2)}) copy-start(bf16[64,1,2048]{2,0,1:T(8,128)(2,1)} %param.7) | copy-start | bytes 786436
  27.4 0.9 copy-start.1
  28.3 0.9 copy-start.3
  29.2 2.2 %copy-start.5 = (bf16[32,1,64,1024]{3,2,1,0:T(8,128)(2,1)S(1)}, bf16[32,1,64,1024]{3,2,1,0:T(8,128)(2,1)}, u32[]{:S(2)}) copy-start(bf16[32,1,64,1024]{3,2,1,0:T(8,128)(2,1)} %param.6) | copy-start | bytes 12582916
  33.2 2.0 %copy-start = (bf16[8,1024,256]{2,1,0:T(8,128)(2,1)}, bf16[8,1024,256]{2,1,0:T(8,128)(2,1)S(1)}, u32[]{:S(2)}) copy-start(bf16[8,1024,256]{2,1,0:T(8,128)(2,1)S(1)} %get-tuple-element.17.flip_hbm) | copy-start | bytes 12582916
  106.3 3.4 %collective-permute-start = (bf16[16,64,128]{2,1,0:T(8,128)(2,1)S(1)}, bf16[16,64,128]{2,1,0:T(8,128)(2,1)S(1)}, u32[]{:S(2)}, u32[]{:S(2)}) collective-permute-start(bf16[16,64,128]{2,1,0:T(8,128)(2,1)S(1)} %get-tuple-element.23), channel_id=1, source_target_pairs={{0,1},{1,0},{2,3},{3,2},{4,5},{5,4},{6,7},{7,6},{8,9},{9,8},{10,11... | collective-permute-start | bytes 786440 | tf_op jit(solution)/shard_map/ppermute | solution.py:253

commit v6 on v5

--- a/solution.py
+++ b/solution.py
@@ -99,9 +99,10 @@
     for b in range(width // BLK):
         cols = slice(b * BLK, (b + 1) * BLK)
         mixed = jnp.zeros((states, BLK), F32)
-        for j in range(DEG):
-            at = slice(j * states, (j + 1) * states)
-            mixed = mixed + dot(pick_ref[at], beta_ref[:, cols]) * dot(choose_ref[at], emis_ref[:, cols])
+        for j in range(0, DEG, 2):
+            at = slice(j * states, (j + 2) * states)
+            both = dot(pick_ref[at], beta_ref[:, cols]) * dot(choose_ref[at], emis_ref[:, cols])
+            mixed = mixed + both[:states] + both[states:]
         mixed_at[b] = mixed.astype(BF)
     load.wait()
     for b in range(width // BLK):

time: 150 us -> 150 us (level)
  no operation moved by 1% of the time
where the time goes in v6:
time: 150 us
  blocking collectives  112 us (75%)
  Pallas kernels  10.9 us (7%)
  local copies, waits for them, and re-layouts  10 us (7%)
  starting transfers between devices  8.96 us (6%)
  waiting for transfers between devices  7.57 us (5%)
    all_to_all x1, blocking collectives, local(): parts = lax.all_to_all(near, ('z2', 'z1', 'zh'), 0, 0)  29.5 us
    all_to_all x1, blocking collectives, local(): parts = lax.all_to_all(halves, ('zh', 'z2', 'z1', 'z0'), 0, 0)  28.3 us
    all_to_all x1, blocking collectives, local(): mixed = lax.all_to_all(copies, PLANE, 0, 0).reshape(width, 256)  17.3 us
    all_gather x1, blocking collectives, local(): pair = lax.all_gather(mine, 'zh', axis=0)  15.9 us
    all_to_all x1, blocking collectives, local(): moved = lax.all_to_all(sum_and_join(parts, keep), PLANE, 0, 0)  10.6 us
    all_to_all x1, blocking collectives, local(): near = near_sum(lax.all_to_all(partial, ('z0', 'c'), 0, 0))  10.5 us
    unnamed x14, local copies, waits for them, and re-layouts  9.18 us
    all_to_all x1, starting transfers between devices, local(): beta = lax.all_to_all(copies_of(pair), PLANE, 0, 0).reshape(256, width)  7.03 us
  transfers between devices with their start and end apart: 2, of which 2 were waited for; matrix products, arithmetic and copies ran while one was open for 2% of the time, Pallas kernels for 1%

profile of v6, /device:TPU:32, one launch (start us, length us, event | category | flops | bytes accessed | tf_op | source)
XLA Modules:
  0.0 149.7 jit_solution(10921566862456495165)
XLA Ops:
  0.0 0.0 copy-start.4
  0.0 0.8 copy-done.4
  0.8 0.1 as_rows.1
  1.0 15.9 %all-gather = bf16[16,2048]{1,0:T(8,128)(2,1)S(1)} all-gather(bf16[8,2048]{1,0:T(8,128)(2,1)S(1)} %as_rows.1), channel_id=2, replica_groups=mesh['y'=4,'x'=4,'zh'=2,'z2'=2,'z1'=2,'z0'=2,'c'=2] {'zh'}, dimensions={0}, use_global_device_ids=true | all-gather | bytes 98304 | tf_op jit(solution)/shard_map/all_gather | solution.py:243
  16.9 1.1 copies.1
  17.9 7.0 %all-to-all-start = ((bf16[16,16,2048]{2,1,0:T(8,128)(2,1)}), bf16[16,16,2048]{2,1,0:T(8,128)(2,1)S(1)}, u32[]{:S(2)}, u32[]{:S(2)}) async-start(bf16[16,16,2048]{2,1,0:T(8,128)(2,1)} %copies.1), calls=%async_computation | async-start | bytes 2097152 | tf_op jit(solution)/shard_map/all_to_all | solution.py:244
  25.0 0.0 copy-start.2
  25.0 0.9 copy.6.succ_ref
  25.9 1.5 copy.7.sets_ref
  27.4 0.0 copy-start.1
  27.4 0.9 copy-done.1
  28.3 0.0 copy-start.3
  28.3 0.9 copy-done.3
  29.2 0.0 copy-start.5
  29.2 2.2 %copy-done.5 = bf16[32,1,64,1024]{3,2,1,0:T(8,128)(2,1)S(1)} copy-done((bf16[32,1,64,1024]{3,2,1,0:T(8,128)(2,1)S(1)}, bf16[32,1,64,1024]{3,2,1,0:T(8,128)(2,1)}, u32[]{:S(2)}) %copy-start.5) | copy-done | bytes 4194328
  31.4 1.8 %tables.1 = (bf16[2048,256]{1,0:T(8,128)(2,1)S(1)}, bf16[2048,64]{1,0:T(8,128)(2,1)S(1)}, bf16[8,128,256]{2,1,0:T(8,128)(2,1)S(1)}, bf16[8,1024,256]{2,1,0:T(8,128)(2,1)S(1)}) custom-call(s32[1]{0:T(128)} %bitcast.3.place_ref, s32[256,8]{1,0:T(8,128)S(1)} %copy.6.succ_ref, s32[256,8]{1,0:T(8,128)S(1)} %copy-done.3, bf16[64,2048]{1,0:T(8,128)(2,1)S(1)} %bitcast.11, ...), custom_call_target="tpu_custom_call" | custom-call | flops 2147483648 | bytes 12582912 | tf_op jit(solution)/shard_map/tables/pallas_call | solution.py:79
  33.2 0.0 copy-start
  33.2 1.9 %copy-done = bf16[8,1024,256]{2,1,0:T(8,128)(2,1)} copy-done((bf16[8,1024,256]{2,1,0:T(8,128)(2,1)}, bf16[8,1024,256]{2,1,0:T(8,128)(2,1)S(1)}, u32[]{:S(2)}) %copy-start) | copy-done | bytes 4194328
  35.1 6.1 %all-to-all-done = bf16[16,16,2048]{2,1,0:T(8,128)(2,1)S(1)} async-done(((bf16[16,16,2048]{2,1,0:T(8,128)(2,1)}), bf16[16,16,2048]{2,1,0:T(8,128)(2,1)S(1)}, u32[]{:S(2)}, u32[]{:S(2)}) %all-to-all-start) | async-done | bytes 1048608 | tf_op jit(solution)/shard_map/all_to_all | solution.py:244
  41.2 0.0 copy-done.2
  41.2 5.8 %mix_multiply.1 = (bf16[4,256,256]{2,1,0:T(8,128)(2,1)S(1)}, bf16[8,1024,256]{2,1,0:T(8,128)(2,1)S(1)}) custom-call(bf16[256,2048]{1,0:T(8,128)(2,1)S(1)} %bitcast.9, bf16[2048,256]{1,0:T(8,128)(2,1)S(1)} %get-tuple-element.15.pick_ref, bf16[2048,64]{1,0:T(8,128)(2,1)S(1)} %get-tuple-element.16.choose_ref, bf16[64,2048]{1,0:T(8,128)(2,1)S(1)} %bitcast.12, ...), custom_call_target="tpu_custom_call" | custom-call | tf_op jit(solution)/shard_map/mix_multiply/pallas_call | solution.py:120
  47.1 10.5 %all_to_all.30.parts_ref = bf16[4,256,256]{2,1,0:T(8,128)(2,1)S(1)} all-to-all(bf16[4,256,256]{2,1,0:T(8,128)(2,1)S(1)} %get-tuple-element.18), channel_id=1, replica_groups=mesh['y'=4,'x'=4,'zh'=2,'z2'=2,'z1'=2,'z0'=2,'c'=2] {'z0','c'}, dimensions={0} | all-to-all | bytes 1048576 | tf_op jit(solution)/shard_map/all_to_all | solution.py:248
  57.6 0.1 near_sum.1
  57.6 29.5 %all_to_all.31.parts_ref = bf16[8,64,256]{2,1,0:T(8,128)(2,1)S(1)} all-to-all(bf16[8,64,256]{2,1,0:T(8,128)(2,1)S(1)} %near_sum.1), channel_id=1, replica_groups=mesh['y'=4,'x'=4,'zh'=2,'z2'=2,'z1'=2,'z0'=2,'c'=2] {'z2','z1','zh'}, dimensions={0} | all-to-all | bytes 524288 | tf_op jit(solution)/shard_map/all_to_all | solution.py:249
  87.1 0.7 sum_mix.1
  87.8 17.3 %all_to_all.32 = bf16[16,128,256]{2,1,0:T(8,128)(2,1)S(1)} all-to-all(bf16[16,128,256]{2,1,0:T(8,128)(2,1)S(1)} %get-tuple-element.20), channel_id=1, replica_groups=mesh['y'=4,'x'=4,'zh'=2,'z2'=2,'z1'=2,'z0'=2,'c'=2] {'y','x'}, dimensions={0} | all-to-all | bytes 2097152 | tf_op jit(solution)/shard_map/all_to_all | solution.py:251
  105.1 1.2 multiply.1
  106.3 1.9 %collective-permute-start = (bf16[16,64,128]{2,1,0:T(8,128)(2,1)S(1)}, bf16[16,64,128]{2,1,0:T(8,128)(2,1)S(1)}, u32[]{:S(2)}, u32[]{:S(2)}) collective-permute-start(bf16[16,64,128]{2,1,0:T(8,128)(2,1)S(1)} %get-tuple-element.23), channel_id=1, source_target_pairs={{0,1},{1,0},{2,3},{3,2},{4,5},{5,4},{6,7},{7,6},{8,9},{9,8},{10,11... | collective-permute-start | bytes 786440 | tf_op jit(solution)/shard_map/ppermute | solution.py:254
  108.2 1.5 %collective-permute-done = bf16[16,64,128]{2,1,0:T(8,128)(2,1)S(1)} collective-permute-done((bf16[16,64,128]{2,1,0:T(8,128)(2,1)S(1)}, bf16[16,64,128]{2,1,0:T(8,128)(2,1)S(1)}, u32[]{:S(2)}, u32[]{:S(2)}) %collective-permute-start) | collective-permute-done | bytes 262176 | tf_op jit(solution)/shard_map/ppermute | solution.py:254
  109.7 0.1 add_convert_fusion
  109.8 28.3 %all_to_all.33.parts_ref = bf16[16,64,128]{2,1,0:T(8,128)(2,1)S(1)} all-to-all(bf16[16,64,128]{2,1,0:T(8,128)(2,1)S(1)} %add_convert_fusion), channel_id=1, replica_groups=mesh['y'=4,'x'=4,'zh'=2,'z2'=2,'z1'=2,'z0'=2,'c'=2] {'zh','z2','z1','z0'}, dimensions={0} | all-to-all | bytes 524288 | tf_op jit(solution)/shard_map/all_to_all | solution.py:255
  138.1 0.1 sum_join.1
  138.2 10.6 %all_to_all.34 = bf16[16,8,256]{2,1,0:T(8,128)(2,1)S(1)} all-to-all(bf16[16,8,256]{2,1,0:T(8,128)(2,1)S(1)} %sum_join.1), channel_id=1, replica_groups=mesh['y'=4,'x'=4,'zh'=2,'z2'=2,'z1'=2,'z0'=2,'c'=2] {'y','x'}, dimensions={0} | all-to-all | bytes 131072 | tf_op jit(solution)/shard_map/all_to_all | solution.py:256
  148.9 0.1 reshape.26
  149.0 0.8 copy.8
Async XLA Ops:
  0.0 0.8 copy-start.4
  17.9 23.3 %all-to-all-start = ((bf16[16,16,2048]{2,1,0:T(8,128)(2,1)}), bf16[16,16,2048]{2,1,0:T(8,128)(2,1)S(1)}, u32[]{:S(2)}, u32[]{:S(2)}) async-start(bf16[16,16,2048]{2,1,0:T(8,128)(2,1)} %copies.1), calls=%async_computation | async-start | bytes 2097152 | tf_op jit(solution)/shard_map/all_to_all | solution.py:244
  25.0 16.2 %copy-start.2 = (bf16[64,1,2048]{2,0,1:T(8,128)(2,1)S(1)}, bf16[64,1,2048]{2,0,1:T(8,128)(2,1)}, u32[]{:S(2)}) copy-start(bf16[64,1,2048]{2,0,1:T(8,128)(2,1)} %param.7) | copy-start | bytes 786436
  27.4 0.9 copy-start.1
  28.3 0.9 copy-start.3
  29.2 2.2 %copy-start.5 = (bf16[32,1,64,1024]{3,2,1,0:T(8,128)(2,1)S(1)}, bf16[32,1,64,1024]{3,2,1,0:T(8,128)(2,1)}, u32[]{:S(2)}) copy-start(bf16[32,1,64,1024]{3,2,1,0:T(8,128)(2,1)} %param.6) | copy-start | bytes 12582916
  33.2 2.0 %copy-start = (bf16[8,1024,256]{2,1,0:T(8,128)(2,1)}, bf16[8,1024,256]{2,1,0:T(8,128)(2,1)S(1)}, u32[]{:S(2)}) copy-start(bf16[8,1024,256]{2,1,0:T(8,128)(2,1)S(1)} %get-tuple-element.17.flip_hbm) | copy-start | bytes 12582916
  106.3 3.4 %collective-permute-start = (bf16[16,64,128]{2,1,0:T(8,128)(2,1)S(1)}, bf16[16,64,128]{2,1,0:T(8,128)(2,1)S(1)}, u32[]{:S(2)}, u32[]{:S(2)}) collective-permute-start(bf16[16,64,128]{2,1,0:T(8,128)(2,1)S(1)} %get-tuple-element.23), channel_id=1, source_target_pairs={{0,1},{1,0},{2,3},{3,2},{4,5},{5,4},{6,7},{7,6},{8,9},{9,8},{10,11... | collective-permute-start | bytes 786440 | tf_op jit(solution)/shard_map/ppermute | solution.py:254
